TPU v7x, 128 devices: a whole 4x4x4 slice. The times are simulated.
128 devices in a mesh: sample: 8 (over y_lo, z), mp: 16 (over x, y_hi, core).
Axes of the slice: x: 4, y: 4 (y_hi: 2, y_lo: 2; y = y_hi * 2 + y_lo), z: 4, core: 2. Of those that a mesh axis runs over, the one named last changes fastest.
Arguments:
- volumes: bfloat16 [64, 8, 4096], P('mp', 'sample'), may hold values from -6 to 6
- w_first: bfloat16 [128, 1728], P('mp'), may hold values from -0.15625 to 0.15625
- w_second: bfloat16 [256, 3456], P('mp'), may hold values from -0.109375 to 0.109375
- cotangent: bfloat16 [256, 8, 4096], P('mp', 'sample'), may hold values from -6 to 6
Outputs:
- features: bfloat16 [256, 8, 4096], P('mp', 'sample')
- input_grad: bfloat16 [64, 8, 4096], P('mp', 'sample')
- grad_first: float32 [128, 1728], P('mp')
- grad_second: float32 [256, 3456], P('mp')
All inputs are finite; a program needn't handle non-finite values.
Results may differ from a plain program's by a relative error of at most 0.024.
Values may be sent and summed in bfloat16 or wider, within the bound.
A program may use at most 64 MiB of HBM per device.

v0:
```python
import math

import jax
import jax.numpy as jnp
from jax import lax
from jax.sharding import PartitionSpec as P

SIDE = 16


def in_order(blocks, dim):
    lengths = list(blocks.shape[1:])
    lengths[dim] *= blocks.shape[0]
    return jnp.moveaxis(blocks, 0, dim).reshape(lengths)


def gather_packed(arrays, axis, dims):
    vector = jnp.concatenate([a.reshape(-1) for a in arrays])
    lines, at, finished = (lax.all_gather(vector, axis), 0, [])
    for a, dim in zip(arrays, dims):
        blocks = lines[:, at : at + a.size].reshape(-1, *a.shape)
        finished.append(in_order(blocks, dim))
        at += a.size
    return tuple(finished)


def extended(array, sides, width):
    for axis, dim in sides:
        size, length = (lax.axis_size(axis), array.shape[dim])
        up = [(i, (i + 1) % size) for i in range(size - 1)]
        down = [(j, i) for i, j in up]
        last = lax.slice_in_dim(array, length - width, length, axis=dim)
        initial = lax.slice_in_dim(array, 0, width, axis=dim)
        before = lax.ppermute(last, axis, up)
        after = lax.ppermute(initial, axis, down)
        array = jnp.concatenate([before, array, after], axis=dim)
    return array


def split_up(array, dim, length):
    before, after = (array.shape[:dim], array.shape[dim + 1 :])
    return jnp.moveaxis(array.reshape(*before, length, -1, *after), dim, 0)


def sum_together(arrays, axis, dims):
    length = lax.axis_size(axis)
    blocks = [split_up(a, dim, length) for a, dim in zip(arrays, dims)]
    lines = jnp.concatenate([b.reshape(length, -1) for b in blocks], axis=1)
    extent = max(16, -(-lines.shape[1] // 1024) * 8)
    lines = jnp.pad(lines, ((0, 0), (0, extent * 128 - lines.shape[1]))).reshape(-1, 128)
    vector, at, finished = (lax.psum_scatter(lines, axis, tiled=True).reshape(-1), 0, [])
    for b in blocks:
        part = b[0]
        finished.append(vector[at : at + part.size].reshape(part.shape))
        at += part.size
    return tuple(finished)


def from_everyone(array, axis):
    length = lax.axis_size(axis)
    return lax.all_to_all(
        jnp.broadcast_to(array[None], (length, *array.shape)), axis, 0, 0, tiled=True
    )


def of_everyone(array, axis):
    return from_everyone(array, axis).astype(jnp.float32).sum(axis=0)


def to_grid(array_in):
    planes = array_in.shape[2] // (SIDE * SIDE)
    return array_in.reshape(array_in.shape[0], array_in.shape[1], planes, SIDE, SIDE)


def conv_forward(grid_in, weights, depth_pad):
    filters = weights.shape[0]
    kernel = weights.reshape(filters, 3, 3, 3, grid_in.shape[0])
    output = lax.conv_general_dilated(
        grid_in,
        kernel,
        (1, 1, 1),
        ((depth_pad, depth_pad), (1, 1), (1, 1)),
        dimension_numbers=("CNDHW", "ODHWI", "CNDHW"),
        preferred_element_type=jnp.float32,
    )
    return output.reshape(filters, grid_in.shape[1], -1)


def conv_data(grid_delta, weights, channels, depth_pad):
    kernel = weights.reshape(weights.shape[0], 3, 3, 3, channels)[:, ::-1, ::-1, ::-1, :]
    output = lax.conv_general_dilated(
        grid_delta,
        kernel,
        (1, 1, 1),
        ((depth_pad, depth_pad), (1, 1), (1, 1)),
        dimension_numbers=("CNDHW", "IDHWO", "CNDHW"),
        preferred_element_type=jnp.float32,
    )
    return output.reshape(channels, grid_delta.shape[1], -1)


def conv_weight(grid_in, grid_delta, depth_pad):
    output = lax.conv_general_dilated(
        grid_in,
        grid_delta,
        (1, 1, 1),
        ((depth_pad, depth_pad), (1, 1), (1, 1)),
        dimension_numbers=("NCDHW", "OIDHW", "NCDHW"),
        preferred_element_type=jnp.float32,
    )
    return jnp.transpose(output, (1, 2, 3, 4, 0)).reshape(grid_delta.shape[0], 27, grid_in.shape[0])


def silu_slope(values):
    sigmoid_v = jax.nn.sigmoid(values)
    return sigmoid_v * (1.0 + values * (1.0 - sigmoid_v))


def local(volumes, w_first, w_second, cotangent):
    in_channels = w_first.shape[1] // 27
    mid_channels = w_second.shape[1] // 27
    batch_here = volumes.shape[1]
    cells = volumes.shape[2]
    grad_scale = 1.0 / math.sqrt(lax.axis_size("sample") * batch_here * cells)
    volume_slab, cotangent_slab = (
        lax.all_to_all(volumes, "mp", split_axis=2, concat_axis=0, tiled=True),
        lax.all_to_all(cotangent, "mp", split_axis=2, concat_axis=0, tiled=True),
    )
    first_all, second_all = gather_packed((w_first, w_second), "mp", (0, 0))
    volume_pad = extended(to_grid(volume_slab), (("mp", 2),), 1)
    pre_first = conv_forward(volume_pad, first_all, 0)
    hidden = jax.nn.silu(pre_first).astype(jnp.bfloat16)
    hidden_pad = extended(to_grid(hidden), (("mp", 2),), 1)
    pre_second = conv_forward(hidden_pad, second_all, 0)
    feature_slab = jax.nn.silu(pre_second).astype(jnp.bfloat16)
    features = lax.all_to_all(feature_slab, "mp", split_axis=0, concat_axis=2, tiled=True)
    delta_second = (cotangent_slab.astype(jnp.float32) * silu_slope(pre_second)).astype(
        jnp.bfloat16
    )
    delta_second_grid = to_grid(delta_second)
    grad_second = conv_weight(hidden_pad, delta_second_grid, 0).reshape(second_all.shape[0], -1)
    delta_second_pad = extended(delta_second_grid, (("mp", 2),), 1)
    grad_hidden = conv_data(delta_second_pad, second_all, mid_channels, 0)
    delta_first = (grad_hidden * silu_slope(pre_first)).astype(jnp.bfloat16)
    delta_first_grid = to_grid(delta_first)
    delta_first_pad = extended(delta_first_grid, (("mp", 2),), 1)
    grad_volume_slab = conv_data(delta_first_pad, first_all, in_channels, 0).astype(jnp.bfloat16)
    input_grad = lax.all_to_all(grad_volume_slab, "mp", split_axis=0, concat_axis=2, tiled=True)
    grad_first = conv_weight(volume_pad, delta_first_grid, 0).reshape(first_all.shape[0], -1)
    share_first, share_second = tuple(
        (
            part.astype(jnp.float32)
            for part in sum_together(
                (grad_first.astype(jnp.bfloat16), grad_second.astype(jnp.bfloat16)), "mp", (0, 0)
            )
        )
    )
    total_first, total_second = (
        of_everyone(share_first.astype(jnp.bfloat16), "sample").astype(jnp.float32),
        of_everyone(share_second.astype(jnp.bfloat16), "sample").astype(jnp.float32),
    )
    return (features, input_grad, total_first * grad_scale, total_second * grad_scale)


def solution(mesh):
    return jax.shard_map(
        local,
        mesh=mesh,
        in_specs=(P("mp", "sample", None), P("mp", None), P("mp", None), P("mp", "sample", None)),
        out_specs=(P("mp", "sample", None), P("mp", "sample", None), P("mp", None), P("mp", None)),
        check_vma=False,
    )
```

profile of v0, /device:TPU:0, one launch (start us, length us, event | category | flops | bytes accessed | tf_op | source)
XLA Modules:
  0.0 290.8 jit_solution(7775857723825258540)
XLA Ops:
  7.2 1.1 reshape.147
  10.0 4.3 %copy.227 = bf16[4,1,4096]{0,1,2:T(2,128)(2,1)S(1)} copy(bf16[4,1,4096]{2,0,1:T(4,128)(2,1)} %param.4) | data formatting | bytes 65536 | tf_op args[0]
  14.8 22.4 %reduce.1 = bf16[4096,4]{1,0:T(8,128)(2,1)S(1)} reduce(bf16[4096,1,4]{2,1,0:T(2,128)(2,1)S(1)} %bitcast.115, bf16[]{:T(256)} %broadcast.144), dimensions={1}, to_apply=%bitcast.97.reduce_sub_computation | reduce | bytes 65538
  37.2 2.0 reshape.225
  39.2 14.6 %all_to_all.70 = bf16[16,2,512]{2,1,0:T(2,128)(2,1)S(1)} all-to-all(bf16[16,2,512]{2,1,0:T(2,128)(2,1)S(1)} %reshape.225), channel_id=1, replica_groups=mesh['sample'=8,'mp'=16] {'mp'}, dimensions={0} | all-to-all | bytes 65536 | tf_op jit(solution)/shard_map/all_to_all | solution.py:126
  53.8 2.7 reshape.226
  56.5 2.0 copy.228
  58.8 1.3 collective-permute-start.1
  60.1 4.0 %collective-permute-start = (bf16[64,1,1,16,16]{4,3,0,2,1:T(8,128)(2,1)S(1)}, bf16[64,1,1,16,16]{4,3,0,2,1:T(8,128)(2,1)}, u32[]{:S(2)}, u32[]{:S(2)}) collective-permute-start(bf16[64,1,1,16,16]{4,3,0,2,1:T(8,128)(2,1)S(1)} %reshape.145), channel_id=1, source_target_pairs={{0,1},{1,2},{2,3},{3,4},{4,5},{5,6},{6,7},{7,8},{8,9},{9,10},{10,1... | collective-permute-start | bytes 98312 | tf_op jit(solution)/shard_map/ppermute | solution.py:34
  64.1 2.7 copy.244
  66.8 22.4 %reduce.3 = bf16[4096,16]{1,0:T(8,128)(2,1)S(1)} reduce(bf16[4096,1,16]{2,1,0:T(2,128)(2,1)S(1)} %bitcast.118, bf16[]{:T(256)} %broadcast.144), dimensions={1}, to_apply=%bitcast.99.reduce_sub_computation | reduce | bytes 262146
  89.3 1.8 reshape.229
  91.0 5.5 %all-to-all-start.2 = ((bf16[16,2,2048]{2,1,0:T(2,128)(2,1)}), bf16[16,2,2048]{2,1,0:T(2,128)(2,1)S(1)}, u32[]{:S(2)}, u32[]{:S(2)}) async-start(bf16[16,2,2048]{2,1,0:T(2,128)(2,1)} %reshape.229), calls=%async_computation.2 | async-start | bytes 262144 | tf_op jit(solution)/shard_map/all_to_all | solution.py:127
  96.6 1.2 maximum_bitcast_fusion
  101.5 2.9 %all-to-all-done.2 = bf16[16,2,2048]{2,1,0:T(2,128)(2,1)S(1)} async-done(((bf16[16,2,2048]{2,1,0:T(2,128)(2,1)}), bf16[16,2,2048]{2,1,0:T(2,128)(2,1)S(1)}, u32[]{:S(2)}, u32[]{:S(2)}) %all-to-all-start.2) | async-done | bytes 131104 | tf_op jit(solution)/shard_map/all_to_all | solution.py:127
  104.5 3.9 %reshape.230 = bf16[4096,1,16]{2,1,0:T(2,128)(2,1)} reshape(bf16[16,2,2048]{2,1,0:T(2,128)(2,1)S(1)} %all-to-all-done.2) | data formatting | bytes 262144
  108.4 2.5 copy.312
  111.7 2.0 reshape_reshape_reshape.8
  113.7 1.9 copy.233
  115.6 2.6 multiply_convert_fusion
  118.3 1.3 collective-permute-start.3
  119.6 15.1 %collective-permute-start.2 = (bf16[128,1,1,16,16]{0,1,4,3,2:T(2,128)(2,1)S(1)}, bf16[128,1,1,16,16]{0,1,4,3,2:T(2,128)(2,1)S(1)}, u32[]{:S(2)}, u32[]{:S(2)}) collective-permute-start(bf16[128,1,1,16,16]{0,1,4,3,2:T(2,128)(2,1)S(1)} %bitcast.132), channel_id=1, source_target_pairs={{0,1},{1,2},{2,3},{3,4},{4,5},{5,6},{6,7},{7,8},{8,9},{9,10},{10,1... | collective-permute-start | bytes 196616 | tf_op jit(solution)/shard_map/ppermute | solution.py:34
  134.8 3.3 %bitcast_convert_fusion = f32[16,1,4096]{0,1,2:T(1,128)} fusion(bf16[4096,1,16]{2,1,0:T(2,128)(2,1)S(1)} %copy-done), kind=kLoop, calls=%fused_computation.111 | loop fusion | flops 65536 | bytes 393216 | tf_op jit(solution)/shard_map/convert_element_type | solution.py:137
  138.0 2.2 copy.245
  140.2 2.0 reshape.192
  142.2 2.5 copy.248
  144.7 1.3 slice.35
  146.0 3.7 %reshape_reshape_reshape.9 = bf16[256,3,3,3,128]{4,3,2,1,0:T(4,128)(2,1)S(1)} reshape(bf16[16,55296]{1,0:T(8,128)(2,1)} %slice.35) | data formatting | bytes 3538944 | tf_op jit(solution)/shard_map/reshape;reshape;reshape | solution.py:77
  152.0 1.3 collective-permute-start.5
  153.3 5.3 %collective-permute-start.4 = (bf16[256,1,1,16,16]{0,4,3,2,1:T(8,128)(2,1)S(1)}, bf16[256,1,1,16,16]{0,4,3,2,1:T(8,128)(2,1)S(1)}, u32[]{:S(2)}, u32[]{:S(2)}) collective-permute-start(bf16[256,1,1,16,16]{0,4,3,2,1:T(8,128)(2,1)S(1)} %fusion.61), channel_id=1, source_target_pairs={{0,1},{1,2},{2,3},{3,4},{4,5},{5,6},{6,7},{7,8},{8,9},{9,10},{10,1... | collective-permute-start | bytes 393224 | tf_op jit(solution)/shard_map/ppermute | solution.py:34
  158.7 3.5 %convolution_convert_fusion = bf16[256,3,3,3,128]{0,4,3,2,1:T(8,128)(2,1)} fusion(bf16[256,1,1,16,16]{0,4,3,2,1:T(8,128)(2,1)S(1)} %fusion.61, bf16[128,1,1,16,16]{0,1,4,3,2:T(2,128)(2,1)S(1)} %collective-permute-done.3, bf16[128,1,1,16,16]{0,1,4,3,2:T(2,128)(2,1)S(1)} %bitcast.134, bf16[128,1,1,16,16]{0,1,4,3,2:T(2,128)(2,1)S(1)} %collective-permute-done.2), kind=kOutput, calls=%fused_computation.8 | convolution fusion | flops 417497088 | bytes 2097152 | tf_op jit(solution)/shard_map/transpose | solution.py:111
  162.2 4.1 %copy.270 = bf16[256,3,3,3,128]{4,3,2,1,0:T(4,128)(2,1)S(1)} copy(bf16[256,3,3,3,128]{0,4,3,2,1:T(8,128)(2,1)} %convolution_convert_fusion) | data formatting | bytes 3538944 | tf_op jit(solution)/shard_map/convert_element_type | solution.py:154
  166.3 2.6 convert_element_type.103
  169.4 1.1 copy-done.2
  170.6 1.5 fusion.18
  174.0 1.0 convert_element_type.101
  175.0 1.6 fusion.2
  176.7 2.1 reshape.149
  179.1 1.3 collective-permute-start.7
  180.4 5.8 %collective-permute-start.6 = (bf16[128,1,1,16,16]{0,3,4,1,2:T(8,128)(2,1)S(1)}, bf16[128,1,1,16,16]{0,3,4,1,2:T(8,128)(2,1)S(1)}, u32[]{:S(2)}, u32[]{:S(2)}) collective-permute-start(bf16[128,1,1,16,16]{0,3,4,1,2:T(8,128)(2,1)S(1)} %slice_bitcast_fusion.2), channel_id=1, source_target_pairs={{0,1},{1,2},{2,3},{3,4},{4,5},{5,6},{6,7},{7,8},{8,9},{9,10},{10,1... | collective-permute-start | bytes 196616 | tf_op jit(solution)/shard_map/ppermute | solution.py:34
  187.8 9.9 %all-to-all-start.1 = ((bf16[16,2,2048]{2,1,0:T(2,128)(2,1)}), bf16[16,2,2048]{2,1,0:T(2,128)(2,1)S(1)}, u32[]{:S(2)}, u32[]{:S(2)}) async-start(bf16[16,2,2048]{2,1,0:T(2,128)(2,1)} %reshape.227), calls=%async_computation.1 | async-start | bytes 262144 | tf_op jit(solution)/shard_map/all_to_all | solution.py:136
  200.2 5.4 %all-to-all-done.1 = bf16[16,2,2048]{2,1,0:T(2,128)(2,1)S(1)} async-done(((bf16[16,2,2048]{2,1,0:T(2,128)(2,1)}), bf16[16,2,2048]{2,1,0:T(2,128)(2,1)S(1)}, u32[]{:S(2)}, u32[]{:S(2)}) %all-to-all-start.1) | async-done | bytes 131104 | tf_op jit(solution)/shard_map/all_to_all | solution.py:136
  205.6 3.5 %all-to-all-start.3 = ((bf16[16,2,512]{2,1,0:T(2,128)(2,1)}), bf16[16,2,512]{2,1,0:T(2,128)(2,1)S(1)}, u32[]{:S(2)}, u32[]{:S(2)}) async-start(bf16[16,2,512]{2,1,0:T(2,128)(2,1)} %reshape.231), calls=%async_computation.3 | async-start | bytes 65536 | tf_op jit(solution)/shard_map/all_to_all | solution.py:148
  209.1 46.0 %reduce-scatter.2.cloned.1.call-done = bf16[544,128]{1,0:T(8,128)(2,1)} async-done(((bf16[8704,128]{1,0:T(8,128)(2,1)}), bf16[544,128]{1,0:T(8,128)(2,1)}) %reduce-scatter.2.cloned.1.call-update) | async-done | bytes 139280 | tf_op jit(solution)/shard_map/reduce_scatter | solution.py:51
  256.7 4.5 %all-to-all-start.4 = ((bf16[8,8,1728]{2,1,0:T(8,128)(2,1)}), bf16[8,8,1728]{2,1,0:T(8,128)(2,1)S(1)}, u32[]{:S(2)}, u32[]{:S(2)}) async-start(bf16[8,8,1728]{2,1,0:T(8,128)(2,1)} %broadcast_in_dim.17), calls=%async_computation.5 | async-start | bytes 458752 | tf_op jit(solution)/shard_map/all_to_all | solution.py:61
  262.4 6.0 %all-to-all-done.4 = bf16[8,8,1728]{2,1,0:T(8,128)(2,1)S(1)} async-done(((bf16[8,8,1728]{2,1,0:T(8,128)(2,1)}), bf16[8,8,1728]{2,1,0:T(8,128)(2,1)S(1)}, u32[]{:S(2)}, u32[]{:S(2)}) %all-to-all-start.4) | async-done | bytes 221216 | tf_op jit(solution)/shard_map/all_to_all | solution.py:61
  269.4 3.5 %all-to-all-start.5 = ((bf16[8,16,3456]{2,1,0:T(8,128)(2,1)}), bf16[8,16,3456]{2,1,0:T(8,128)(2,1)S(1)}, u32[]{:S(2)}, u32[]{:S(2)}) async-start(bf16[8,16,3456]{2,1,0:T(8,128)(2,1)} %broadcast_in_dim.19), calls=%async_computation.6 | async-start | bytes 1769472 | tf_op jit(solution)/shard_map/all_to_all | solution.py:61
  275.2 7.7 %all-to-all-done.5 = bf16[8,16,3456]{2,1,0:T(8,128)(2,1)S(1)} async-done(((bf16[8,16,3456]{2,1,0:T(8,128)(2,1)}), bf16[8,16,3456]{2,1,0:T(8,128)(2,1)S(1)}, u32[]{:S(2)}, u32[]{:S(2)}) %all-to-all-start.5) | async-done | bytes 884768 | tf_op jit(solution)/shard_map/all_to_all | solution.py:61
  (111 shorter events, 23.0 us)
Async XLA Ops:
  7.2 101.2 %all-gather.4.cloned.1.call-start = ((), (), s32[]{:S(2)}) async-start(), calls=%async_computation.8 | async-start | bytes 4700160 | tf_op jit(solution)/shard_map/all_gather | solution.py:19
  53.8 10.3 %copy-start.8 = (bf16[16,1,4096]{2,0,1:T(8,128)(2,1)S(1)}, bf16[16,1,4096]{2,0,1:T(8,128)(2,1)}, u32[]{:S(2)}) copy-start(bf16[16,1,4096]{2,0,1:T(8,128)(2,1)} %param.7) | copy-start | bytes 393220
  58.8 37.7 %collective-permute-start.1 = (bf16[64,1,1,16,16]{4,3,0,2,1:T(8,128)(2,1)S(1)}, bf16[64,1,1,16,16]{4,3,0,2,1:T(8,128)(2,1)}, u32[]{:S(2)}, u32[]{:S(2)}) collective-permute-start(bf16[64,1,1,16,16]{4,3,0,2,1:T(8,128)(2,1)S(1)} %reshape.145), channel_id=1, source_target_pairs={{1,0},{2,1},{3,2},{4,3},{5,4},{6,5},{7,6},{8,7},{9,8},{10,9},{11,1... | collective-permute-start | bytes 98312 | tf_op jit(solution)/shard_map/ppermute | solution.py:35
  60.1 36.5 %collective-permute-start = (bf16[64,1,1,16,16]{4,3,0,2,1:T(8,128)(2,1)S(1)}, bf16[64,1,1,16,16]{4,3,0,2,1:T(8,128)(2,1)}, u32[]{:S(2)}, u32[]{:S(2)}) collective-permute-start(bf16[64,1,1,16,16]{4,3,0,2,1:T(8,128)(2,1)S(1)} %reshape.145), channel_id=1, source_target_pairs={{0,1},{1,2},{2,3},{3,4},{4,5},{5,6},{6,7},{7,8},{8,9},{9,10},{10,1... | collective-permute-start | bytes 98312 | tf_op jit(solution)/shard_map/ppermute | solution.py:34
  91.0 13.5 %all-to-all-start.2 = ((bf16[16,2,2048]{2,1,0:T(2,128)(2,1)}), bf16[16,2,2048]{2,1,0:T(2,128)(2,1)S(1)}, u32[]{:S(2)}, u32[]{:S(2)}) async-start(bf16[16,2,2048]{2,1,0:T(2,128)(2,1)} %reshape.229), calls=%async_computation.2 | async-start | bytes 262144 | tf_op jit(solution)/shard_map/all_to_all | solution.py:127
  96.5 158.7 %reduce-scatter.2.cloned.1.call-start = ((), (), s32[]{:S(2)}) async-start(), calls=%async_computation.7 | async-start | bytes 2367488 | tf_op jit(solution)/shard_map/reduce_scatter | solution.py:51
  98.7 1.9 copy-start.3
  110.9 4.7 %copy-start.9 = (pred[8,3]{0,1:T(4,128)(4,1)S(1)}, pred[8,3]{0,1:T(4,128)(4,1)}, u32[]{:S(2)}) copy-start(pred[8,3]{0,1:T(4,128)(4,1)} %constant.41) | copy-start | bytes 76
  115.6 19.2 %copy-start = (bf16[4096,1,16]{2,1,0:T(2,128)(2,1)S(1)}, bf16[4096,1,16]{2,1,0:T(2,128)(2,1)}, u32[]{:S(2)}) copy-start(bf16[4096,1,16]{2,1,0:T(2,128)(2,1)} %reshape.230) | copy-start | bytes 393220
  118.3 31.4 %collective-permute-start.3 = (bf16[128,1,1,16,16]{0,1,4,3,2:T(2,128)(2,1)S(1)}, bf16[128,1,1,16,16]{0,1,4,3,2:T(2,128)(2,1)S(1)}, u32[]{:S(2)}, u32[]{:S(2)}) collective-permute-start(bf16[128,1,1,16,16]{0,1,4,3,2:T(2,128)(2,1)S(1)} %bitcast.131), channel_id=1, source_target_pairs={{1,0},{2,1},{3,2},{4,3},{5,4},{6,5},{7,6},{8,7},{9,8},{10,9},{11,1... | collective-permute-start | bytes 196616 | tf_op jit(solution)/shard_map/ppermute | solution.py:35
  119.6 30.1 %collective-permute-start.2 = (bf16[128,1,1,16,16]{0,1,4,3,2:T(2,128)(2,1)S(1)}, bf16[128,1,1,16,16]{0,1,4,3,2:T(2,128)(2,1)S(1)}, u32[]{:S(2)}, u32[]{:S(2)}) collective-permute-start(bf16[128,1,1,16,16]{0,1,4,3,2:T(2,128)(2,1)S(1)} %bitcast.132), channel_id=1, source_target_pairs={{0,1},{1,2},{2,3},{3,4},{4,5},{5,6},{6,7},{7,8},{8,9},{9,10},{10,1... | collective-permute-start | bytes 196616 | tf_op jit(solution)/shard_map/ppermute | solution.py:34
  149.7 2.0 copy-start.1
  152.0 16.9 %collective-permute-start.5 = (bf16[256,1,1,16,16]{0,4,3,2,1:T(8,128)(2,1)S(1)}, bf16[256,1,1,16,16]{0,4,3,2,1:T(8,128)(2,1)S(1)}, u32[]{:S(2)}, u32[]{:S(2)}) collective-permute-start(bf16[256,1,1,16,16]{0,4,3,2,1:T(8,128)(2,1)S(1)} %fusion.61), channel_id=1, source_target_pairs={{1,0},{2,1},{3,2},{4,3},{5,4},{6,5},{7,6},{8,7},{9,8},{10,9},{11,1... | collective-permute-start | bytes 393224 | tf_op jit(solution)/shard_map/ppermute | solution.py:35
  153.3 15.6 %collective-permute-start.4 = (bf16[256,1,1,16,16]{0,4,3,2,1:T(8,128)(2,1)S(1)}, bf16[256,1,1,16,16]{0,4,3,2,1:T(8,128)(2,1)S(1)}, u32[]{:S(2)}, u32[]{:S(2)}) collective-permute-start(bf16[256,1,1,16,16]{0,4,3,2,1:T(8,128)(2,1)S(1)} %fusion.61), channel_id=1, source_target_pairs={{0,1},{1,2},{2,3},{3,4},{4,5},{5,6},{6,7},{7,8},{8,9},{9,10},{10,1... | collective-permute-start | bytes 393224 | tf_op jit(solution)/shard_map/ppermute | solution.py:34
  168.9 1.7 copy-start.2
  168.9 1.7 copy-start.10
  170.6 1.6 copy-start.5
  170.6 1.6 copy-start.6
  170.6 1.6 copy-start.7
  178.9 19.0 %copy-start.4 = (bf16[128,3,3,3,64]{0,4,3,2,1:T(8,128)(2,1)S(1)}, bf16[128,3,3,3,64]{0,4,3,2,1:T(8,128)(2,1)}, u32[]{:S(2)}) copy-start(bf16[128,3,3,3,64]{0,4,3,2,1:T(8,128)(2,1)} %copy.233) | copy-start | bytes 1327108
  179.1 18.5 %collective-permute-start.7 = (bf16[128,1,1,16,16]{0,3,4,1,2:T(8,128)(2,1)S(1)}, bf16[128,1,1,16,16]{0,3,4,1,2:T(8,128)(2,1)S(1)}, u32[]{:S(2)}, u32[]{:S(2)}) collective-permute-start(bf16[128,1,1,16,16]{0,3,4,1,2:T(8,128)(2,1)S(1)} %slice_bitcast_fusion.2), channel_id=1, source_target_pairs={{1,0},{2,1},{3,2},{4,3},{5,4},{6,5},{7,6},{8,7},{9,8},{10,9},{11,1... | collective-permute-start | bytes 196616 | tf_op jit(solution)/shard_map/ppermute | solution.py:35
  180.4 17.2 %collective-permute-start.6 = (bf16[128,1,1,16,16]{0,3,4,1,2:T(8,128)(2,1)S(1)}, bf16[128,1,1,16,16]{0,3,4,1,2:T(8,128)(2,1)S(1)}, u32[]{:S(2)}, u32[]{:S(2)}) collective-permute-start(bf16[128,1,1,16,16]{0,3,4,1,2:T(8,128)(2,1)S(1)} %slice_bitcast_fusion.2), channel_id=1, source_target_pairs={{0,1},{1,2},{2,3},{3,4},{4,5},{5,6},{6,7},{7,8},{8,9},{9,10},{10,1... | collective-permute-start | bytes 196616 | tf_op jit(solution)/shard_map/ppermute | solution.py:34
  187.8 17.9 %all-to-all-start.1 = ((bf16[16,2,2048]{2,1,0:T(2,128)(2,1)}), bf16[16,2,2048]{2,1,0:T(2,128)(2,1)S(1)}, u32[]{:S(2)}, u32[]{:S(2)}) async-start(bf16[16,2,2048]{2,1,0:T(2,128)(2,1)} %reshape.227), calls=%async_computation.1 | async-start | bytes 262144 | tf_op jit(solution)/shard_map/all_to_all | solution.py:136
  205.6 50.4 %all-to-all-start.3 = ((bf16[16,2,512]{2,1,0:T(2,128)(2,1)}), bf16[16,2,512]{2,1,0:T(2,128)(2,1)S(1)}, u32[]{:S(2)}, u32[]{:S(2)}) async-start(bf16[16,2,512]{2,1,0:T(2,128)(2,1)} %reshape.231), calls=%async_computation.3 | async-start | bytes 65536 | tf_op jit(solution)/shard_map/all_to_all | solution.py:148
  256.7 11.6 %all-to-all-start.4 = ((bf16[8,8,1728]{2,1,0:T(8,128)(2,1)}), bf16[8,8,1728]{2,1,0:T(8,128)(2,1)S(1)}, u32[]{:S(2)}, u32[]{:S(2)}) async-start(bf16[8,8,1728]{2,1,0:T(8,128)(2,1)} %broadcast_in_dim.17), calls=%async_computation.5 | async-start | bytes 458752 | tf_op jit(solution)/shard_map/all_to_all | solution.py:61
  269.4 13.6 %all-to-all-start.5 = ((bf16[8,16,3456]{2,1,0:T(8,128)(2,1)}), bf16[8,16,3456]{2,1,0:T(8,128)(2,1)S(1)}, u32[]{:S(2)}, u32[]{:S(2)}) async-start(bf16[8,16,3456]{2,1,0:T(8,128)(2,1)} %broadcast_in_dim.19), calls=%async_computation.6 | async-start | bytes 1769472 | tf_op jit(solution)/shard_map/all_to_all | solution.py:61
Sparse Core Ops, SparseCore 0:
  10.4 59.8 all-gather.3
  178.9 76.2 reduce-scatter.1
where the time goes:
time: 293 us; the launch traced here: 291 us
  waiting for transfers between devices  68.1 us (23%)
  local copies, waits for them, and re-layouts  64.3 us (22%)
  starting transfers between devices  62.4 us (21%)
  other arithmetic  56 us (19%)
  between operations  15 us (5%)
  blocking collectives  14.6 us (5%)
  matrix products  10.4 us (4%)
    reduce_scatter x1, waiting for transfers between devices, sum_together(): lax.psum_scatter(lines, axis, tiled=True).reshape(-1)  46 us
    unnamed x2, other arithmetic  44.8 us
    ppermute x4, starting transfers between devices, extended(): before = lax.ppermute(last, axis, up)  30.2 us
    unnamed x48, local copies, waits for them, and re-layouts  25.4 us
    all_to_all x1, blocking collectives, local(): lax.all_to_all(volumes, 'mp', split_axis=2, concat_axis=0, tiled=True)  14.6 us
    all_to_all x2, waiting for transfers between devices, from_everyone(): lax.all_to_all(jnp.broadcast_to(array[None], (length, *array.shape)), axi...  13.7 us
    all_to_all x1, starting transfers between devices, local(): lax.all_to_all(feature_slab, 'mp', split_axis=0, concat_axis=2, tiled=True)  9.87 us
    all_to_all x2, starting transfers between devices, from_everyone(): lax.all_to_all(jnp.broadcast_to(array[None], (length, *array.shape)), axi...  8.09 us
  transfers between devices with their start and end apart: 15, of which 5 were waited for; matrix products, arithmetic and copies ran while one was open for 35% of the time, Pallas kernels for 0%

commit v1 on v0

v1 whole, which is shorter than its diff:
```python
import functools
import math

import jax
import jax.numpy as jnp
from jax import lax
from jax.experimental import pallas as pl
from jax.experimental.pallas import tpu as pltpu
from jax.sharding import PartitionSpec as P

MESH = pl.DeviceIdType.MESH
F32 = jnp.float32
BF16 = jnp.bfloat16
PLANE = 256
OWN = 8
HALF = OWN * PLANE
WIDE1 = HALF + 2 * PLANE
WIDE2 = HALF + 4 * PLANE


def at(start, size, unit):
    return pl.ds(pl.multiple_of(start, unit), size)


def plane_at(index, planes=1):
    return at(index * PLANE, planes * PLANE, PLANE)


def place(rows, lanes):
    return lax.broadcasted_iota(jnp.int32, (rows, lanes), 1)


def shifted_x(value, step):
    rows, lanes = value.shape
    x = place(rows, lanes) % 16
    if step > 0:
        return jnp.where(x < 15, pltpu.roll(value, lanes - 1, 1), 0.0)
    return jnp.where(x > 0, pltpu.roll(value, 1, 1), 0.0)


def shifted_y(value, step):
    rows, lanes = value.shape
    cell = place(rows, lanes)
    if step > 0:
        return jnp.where(cell < PLANE - 16, pltpu.roll(value, lanes - 16, 1), 0.0)
    return jnp.where(cell >= 16, pltpu.roll(value, 16, 1), 0.0)


def sigmoid(v):
    return 1.0 / (1.0 + jnp.exp(-v))


def slope(v):
    s = sigmoid(v)
    return s * (1.0 + v * (1.0 - s))


def mm(a, b, ca, cb):
    return lax.dot_general(a, b, (((ca,), (cb,)), ((), ())), preferred_element_type=F32)


def conv_plane(y_ref, rows, p):
    sums = []
    for dy in range(3):
        total = None
        for dz in range(3):
            k = 3 * dz + dy
            part = y_ref[rows * k : rows * (k + 1), plane_at(p + dz)]
            total = part if total is None else total + part
        sums.append(total)
    return sums[1] + shifted_y(sums[0], -1) + shifted_y(sums[2], 1)


def kernel(
    scale, vol, w1, w2, cot, feat, ig_out, g1_out, g2_out,
    vrecv, wb1, wb2, cb, w1s, w2s, vf, v3, y1, pre1, h, h3, y2, fb, fr, dlb, halo2, e2,
    ghb, ghr, d1b, halo1, e1, igb, igr, gsf, gsx, gsr, gp, gpr, gq, g1f, g1x, g1r, g1t, g1b, g1q,
    loc, sib_s, sib_r, vs, vr, hs, hr, gs, gr, is_, ir, ps, pr, qs, qr, g1s, g1rr,
):
    s = lax.axis_index("sample")
    m = lax.axis_index("mp")
    core = m % 2
    chip = m // 2
    sib = chip * 2 + (1 - core)
    waits = []

    def send(src, dst, ssem, rsem, sample, mp):
        c = pltpu.make_async_remote_copy(
            src_ref=src, dst_ref=dst, send_sem=ssem, recv_sem=rsem,
            device_id=(sample, mp), device_id_type=MESH,
        )
        c.start()
        waits.append(c)
        return c

    barrier = pltpu.get_barrier_semaphore()
    for r in range(1, 16):
        pl.semaphore_signal(barrier, inc=1, device_id=(s, (m + r) % 16), device_id_type=MESH)
    for r in range(1, 8):
        pl.semaphore_signal(barrier, inc=1, device_id=((s + r) % 8, m), device_id_type=MESH)

    half = at(core * HALF, HALF, HALF)
    other = at((1 - core) * HALF, HALF, HALF)
    local = [
        pltpu.make_async_copy(vol.at[:, at(core * 1536, WIDE1, PLANE)], vrecv.at[m], loc.at[0]),
        pltpu.make_async_copy(w1, wb1.at[core], loc.at[1]),
        pltpu.make_async_copy(w2, wb2.at[core], loc.at[2]),
        pltpu.make_async_copy(cot.at[:, half], cb.at[core], loc.at[3]),
    ]
    for c in local:
        c.start()
    pl.semaphore_wait(barrier, 22)

    vol_copies = []
    for r in range(1, 16):
        to = (m + r) % 16
        src = vol.at[:, at((to % 2) * 1536, WIDE1, PLANE)]
        vol_copies.append(send(src, vrecv.at[m], vs.at[r - 1], vr.at[r - 1], s, to))
    w1_copy = send(w1, wb1.at[core], sib_s.at[0], sib_r.at[0], s, sib)
    w2_copy = send(w2, wb2.at[core], sib_s.at[1], sib_r.at[1], s, sib)
    cot_copy = send(cot.at[:, other], cb.at[core], sib_s.at[2], sib_r.at[2], s, sib)

    local[1].wait()
    w1_copy.wait_recv()
    w1_all = jnp.concatenate([wb1[0].astype(F32), wb1[1].astype(F32)], axis=0)
    for k in range(9):
        w1s[16 * k : 16 * k + 16, :] = w1_all[:, 192 * k : 192 * k + 192].astype(BF16)
    local[2].wait()
    w2_copy.wait_recv()
    for k in range(9):
        for c in range(2):
            w2s[32 * k + 16 * c : 32 * k + 16 * c + 16, :] = wb2[c, :, 384 * k : 384 * k + 384]
    gp[27:32] = jnp.zeros((5, 16, 128), BF16)
    vf[:, at(core * WIDE1, 2 * PLANE, PLANE)] = jnp.zeros((64, 2 * PLANE), F32)
    local[0].wait()
    for c in vol_copies:
        c.wait_recv()
    for i in range(16):
        vf[4 * i : 4 * i + 4, at((1 - core) * 2 * PLANE, WIDE1, PLANE)] = vrecv[i].astype(F32)

    def stack_v(p, _):
        value = vf[:, plane_at(p)]
        for dx in range(3):
            part = value if dx == 1 else shifted_x(value, dx - 1)
            v3[64 * dx : 64 * dx + 64, plane_at(p)] = part.astype(BF16)
        y1[:, plane_at(p)] = mm(w1s[...], v3[:, plane_at(p)], 1, 0)
        return 0

    lax.fori_loop(0, 12, stack_v, 0)

    rows16 = at(chip * 16, 16, 16)

    def first(p, _):
        value = conv_plane(y1, 16, p)
        pre1[:, plane_at(p)] = value
        z = core * OWN + p - 1
        inside = jnp.logical_and(z >= 0, z < 16)
        hidden = jnp.where(inside, value * sigmoid(value), 0.0)
        h[rows16, plane_at(p)] = hidden.astype(BF16)
        return 0

    lax.fori_loop(0, 10, first, 0)

    h_copies = []
    for r in range(1, 8):
        to = ((chip + r) % 8) * 2 + core
        h_copies.append(send(h.at[rows16], h.at[rows16], hs.at[r - 1], hr.at[r - 1], s, to))
    local[3].wait()
    cot_copy.wait_recv()
    for c in h_copies:
        c.wait_recv()

    def stack_h(p, _):
        value = h[:, plane_at(p)].astype(F32)
        for dx in range(3):
            part = value if dx == 1 else shifted_x(value, dx - 1)
            h3[128 * dx : 128 * dx + 128, plane_at(p)] = part.astype(BF16)
        y2[:, plane_at(p)] = mm(w2s[...], h3[:, plane_at(p)], 1, 0)
        return 0

    lax.fori_loop(0, 10, stack_h, 0)

    def second(p, _):
        value = conv_plane(y2, 32, p)
        sg = sigmoid(value)
        out = (value * sg).astype(BF16)
        fb[0, :, plane_at(p)] = out[:16]
        fb[1, :, plane_at(p)] = out[16:]
        cots = jnp.concatenate([cb[0, :, plane_at(p)], cb[1, :, plane_at(p)]], axis=0)
        delta = cots.astype(F32) * (sg * (1.0 + value * (1.0 - sg)))
        dlb[:, plane_at(p + 1)] = delta.astype(BF16)
        return 0

    lax.fori_loop(0, OWN, second, 0)

    edge = plane_at(OWN - (OWN - 1) * core)
    halo2_copy = send(dlb.at[:, edge], halo2, sib_s.at[3], sib_r.at[3], s, sib)
    feat_copy = send(fb.at[1 - core], fr, sib_s.at[4], sib_r.at[4], s, sib)

    def spread(src, dst, rows):
        def body(p, _):
            value = src[:, plane_at(p)].astype(F32)
            dst[0:rows, plane_at(p)] = shifted_y(value, 1).astype(BF16)
            dst[rows : 2 * rows, plane_at(p)] = value.astype(BF16)
            dst[2 * rows : 3 * rows, plane_at(p)] = shifted_y(value, -1).astype(BF16)
            return 0

        return body

    def halos(src, dst, rows, received):
        value = received[...].astype(F32)
        for p, mine in ((0, core == 1), (OWN + 1, core == 0)):
            src[:, PLANE * p : PLANE * (p + 1)] = jnp.where(mine, value, 0.0).astype(BF16)
            spread(src, dst, rows)(p, 0)

    lax.fori_loop(1, OWN + 1, spread(dlb, e2, 32), 0)
    halo2_copy.wait_recv()
    halos(dlb, e2, 32, halo2)

    def around(e, p):
        return jnp.concatenate([e[:, plane_at(p + 2 - dz)] for dz in range(3)], axis=0)

    def collect(z, rows):
        return z[rows : 2 * rows] + shifted_x(z[:rows], 1) + shifted_x(z[2 * rows :], -1)

    def hidden_grad(p, _):
        z = mm(w2s[...], around(e2, p), 0, 0)
        ghb[:, plane_at(p)] = collect(z, 128).astype(BF16)
        return 0

    lax.fori_loop(0, OWN, hidden_grad, 0)

    gh_copies = []
    for r in range(1, 8):
        to = (chip + r) % 8
        src = ghb.at[at(to * 16, 16, 16)]
        gh_copies.append(send(src, ghr.at[r - 1], gs.at[r - 1], gr.at[r - 1], s, to * 2 + core))

    for dz in range(3):
        part = mm(e2[:, PLANE * (2 - dz) : PLANE * (2 - dz) + HALF], h3[:, PLANE : PLANE + HALF], 1, 1)
        for dy in range(3):
            gsf[3 * dz + dy] = part[32 * dy : 32 * dy + 32]
    mine16 = at(core * 16, 16, 16)
    gsx[...] = gsf[:, at((1 - core) * 16, 16, 16), :].astype(BF16)
    gs_copy = send(gsx, gsr, sib_s.at[5], sib_r.at[5], s, sib)
    feat_copy.wait_recv()
    feat[:, half] = fb[core]
    feat[:, other] = fr[...]
    gs_copy.wait_recv()
    for k in range(9):
        part = (gsf[k, mine16, :] + gsr[k].astype(F32)).astype(BF16)
        for dx in range(3):
            gp[3 * k + dx] = part[:, 128 * dx : 128 * dx + 128]
    gp_copies = []
    for r in range(1, 8):
        to = (s + r) % 8
        gp_copies.append(send(gp.at[pl.ds(4 * to, 4)], gpr.at[r - 1], ps.at[r - 1], pr.at[r - 1], to, m))

    for c in gh_copies:
        c.wait_recv()

    def delta_first(p, _):
        total = ghb[rows16, plane_at(p)].astype(F32)
        for r in range(7):
            total += ghr[r, :, plane_at(p)].astype(F32)
        d1b[:, plane_at(p + 1)] = (total * slope(pre1[:, plane_at(p + 1)])).astype(BF16)
        return 0

    lax.fori_loop(0, OWN, delta_first, 0)
    halo1_copy = send(d1b.at[:, edge], halo1, sib_s.at[6], sib_r.at[6], s, sib)
    lax.fori_loop(1, OWN + 1, spread(d1b, e1, 16), 0)
    halo1_copy.wait_recv()
    halos(d1b, e1, 16, halo1)

    def input_grad(p, _):
        z = mm(w1s[...], around(e1, p), 0, 0)
        value = collect(z, 64)
        for i in range(16):
            igb[i, :, plane_at(p)] = value[4 * i : 4 * i + 4].astype(BF16)
        return 0

    lax.fori_loop(0, OWN, input_grad, 0)

    ig_copies = []
    for r in range(1, 16):
        to = (m + r) % 16
        ig_copies.append(send(igb.at[to], igr.at[r - 1], is_.at[r - 1], ir.at[r - 1], s, to))

    for dz in range(3):
        lanes = slice(PLANE * (2 - dz), PLANE * (2 - dz) + HALF)
        part = mm(e1[:, lanes], v3[:, 2 * PLANE : 2 * PLANE + HALF], 1, 1)
        for dy in range(3):
            g1f[3 * dz + dy] = part[16 * dy : 16 * dy + 16]
    g1x[...] = g1f[:, at((1 - core) * 8, 8, 8), :].astype(BF16)
    g1_copy = send(g1x, g1r, sib_s.at[7], sib_r.at[7], s, sib)

    for c in gp_copies:
        c.wait_recv()
    quarter = pl.ds(4 * s, 4)
    total = gp[quarter].astype(F32)
    for r in range(7):
        total += gpr[r].astype(F32)
    gq[quarter] = (total * scale).astype(BF16)
    gq_copies = []
    for r in range(1, 8):
        to = (s + r) % 8
        gq_copies.append(send(gq.at[quarter], gq.at[quarter], qs.at[r - 1], qr.at[r - 1], to, m))

    g1_copy.wait_recv()
    mine8 = at(core * 8, 8, 8)
    for k in range(9):
        g1t[:, 192 * k : 192 * k + 192] = g1f[k, mine8, :] + g1r[k].astype(F32)
    g1b[...] = g1t[...].astype(BF16)
    g1_copies = []
    for r in range(1, 8):
        to = (s + r) % 8
        g1_copies.append(send(g1b, g1q.at[r - 1], g1s.at[r - 1], g1rr.at[r - 1], to, m))

    for c in ig_copies:
        c.wait_recv()
    same = igb[m].astype(F32)
    for r in range(2, 16, 2):
        same += igr[r - 1].astype(F32)
    ig_out[:, half] = same.astype(BF16)
    across = igr[0].astype(F32)
    for r in range(3, 16, 2):
        across += igr[r - 1].astype(F32)
    ig_out[:, other] = across.astype(BF16)

    for c in gq_copies:
        c.wait_recv()
    for t in range(27):
        g2_out[:, 128 * t : 128 * t + 128] = gq[t].astype(F32)
    for c in g1_copies:
        c.wait_recv()
    total = g1t[...]
    for r in range(7):
        total += g1q[r].astype(F32)
    g1_out[...] = total * scale

    for c in waits:
        c.wait_send()


def local_step(volumes, w_first, w_second, cotangent):
    cells = 2 * HALF
    scale = 1.0 / math.sqrt(lax.axis_size("sample") * volumes.shape[1] * cells)
    V = pltpu.VMEM
    dma = pltpu.SemaphoreType.DMA
    scratch = [
        V((16, 4, WIDE1), BF16), V((2, 8, 1728), BF16), V((2, 16, 3456), BF16), V((2, 16, HALF), BF16),
        V((144, 192), BF16), V((288, 384), BF16), V((64, WIDE2), F32), V((192, WIDE2), BF16),
        V((144, WIDE2), F32), V((16, WIDE1), F32), V((128, WIDE1), BF16), V((384, WIDE1), BF16),
        V((288, WIDE1), F32), V((2, 16, HALF), BF16), V((16, HALF), BF16), V((32, WIDE1), BF16),
        V((32, PLANE), BF16), V((96, WIDE1), BF16),
        V((128, HALF), BF16), V((7, 16, HALF), BF16), V((16, WIDE1), BF16), V((16, PLANE), BF16),
        V((48, WIDE1), BF16), V((16, 4, HALF), BF16), V((15, 4, HALF), BF16),
        V((9, 32, 384), F32), V((9, 16, 384), BF16), V((9, 16, 384), BF16),
        V((32, 16, 128), BF16), V((7, 4, 16, 128), BF16), V((32, 16, 128), BF16),
        V((9, 16, 192), F32), V((9, 8, 192), BF16), V((9, 8, 192), BF16),
        V((8, 1728), F32), V((8, 1728), BF16), V((7, 8, 1728), BF16),
        dma((4,)), dma((8,)), dma((8,)), dma((15,)), dma((15,)), dma((7,)), dma((7,)),
        dma((7,)), dma((7,)), dma((15,)), dma((15,)), dma((7,)), dma((7,)), dma((7,)), dma((7,)),
        dma((7,)), dma((7,)),
    ]
    any_space = pl.BlockSpec(memory_space=pl.ANY)
    vmem = pl.BlockSpec(memory_space=pltpu.VMEM)
    feat, ig, g1, g2 = pl.pallas_call(
        functools.partial(kernel, scale),
        out_shape=(
            jax.ShapeDtypeStruct((16, cells), BF16),
            jax.ShapeDtypeStruct((4, cells), BF16),
            jax.ShapeDtypeStruct((8, 1728), F32),
            jax.ShapeDtypeStruct((16, 3456), F32),
        ),
        in_specs=[any_space] * 4,
        out_specs=(vmem,) * 4,
        scratch_shapes=scratch,
        compiler_params=pltpu.CompilerParams(
            collective_id=0, has_side_effects=True, vmem_limit_bytes=60 * 1024 * 1024
        ),
    )(volumes.reshape(4, cells), w_first, w_second, cotangent.reshape(16, cells))
    return feat.reshape(16, 1, cells), ig.reshape(4, 1, cells), g1, g2


def solution(mesh):
    return jax.shard_map(
        local_step,
        mesh=mesh,
        in_specs=(P("mp", "sample", None), P("mp", None), P("mp", None), P("mp", "sample", None)),
        out_specs=(P("mp", "sample", None), P("mp", "sample", None), P("mp", None), P("mp", None)),
        check_vma=False,
    )
```

time: 293 us -> 66.6 us (0.23)
  the two profiles are of different devices: /device:TPU:0 before, /device:TPU:1 now
where the time goes in v1:
time: 66.6 us; the launch traced here: 66.4 us
  Pallas kernels  62 us (93%)
  local copies, waits for them, and re-layouts  3.76 us (6%)
    pallas_call x1, Pallas kernels, local_step(): pl.pallas_call(functools.partial(kernel, scale), out_shape=(jax.ShapeDtyp...  62 us
    unnamed x10, local copies, waits for them, and re-layouts  3.76 us

profile of v1, /device:TPU:1, one launch (start us, length us, event | category | flops | bytes accessed | tf_op | source)
XLA Modules:
  0.0 66.4 jit_solution(2904784765651912255)
XLA Ops:
  0.6 62.0 %shard_map.75 = (bf16[16,4096]{1,0:T(8,128)(2,1)}, bf16[4,4096]{1,0:T(4,128)(2,1)}, f32[8,1728]{1,0:T(8,128)}, f32[16,3456]{1,0:T(8,128)}) custom-call(bf16[4,4096]{1,0:T(4,128)(2,1)} %bitcast.6, bf16[8,1728]{1,0:T(8,128)(2,1)} %w1.1, bf16[16,3456]{1,0:T(8,128)(2,1)} %w2.1, bf16[16,4096]{1,0:T(8,128)(2,1)} %bitcast.4), custom_call_target="tpu_custom_call" | custom-call | tf_op jit(solution)/shard_map/pallas_call | solution.py:368
  62.6 0.0 copy-start.2
  62.7 0.0 copy-start
  62.7 1.6 %copy.12 = bf16[16,1,4096]{2,0,1:T(8,128)(2,1)} copy(bf16[16,1,4096]{2,0,1:T(8,128)(2,1)} %bitcast.5) | data formatting | bytes 262144
  64.3 0.0 copy-done.2
  64.3 0.0 copy-start.1
  64.3 0.6 copy.13
  64.9 0.2 copy-done.1
  65.1 0.6 copy.14
  65.7 0.0 copy-done
  65.7 0.7 %copy.15 = f32[16,3456]{1,0:T(8,128)} copy(f32[16,3456]{1,0:T(8,128)S(1)} %copy-done) | data formatting | bytes 442368
Async XLA Ops:
  62.6 1.6 %copy-start.2 = (bf16[4,4096]{1,0:T(4,128)(2,1)S(1)}, bf16[4,4096]{1,0:T(4,128)(2,1)}, u32[]{:S(2)}) copy-start(bf16[4,4096]{1,0:T(4,128)(2,1)} %get-tuple-element.9) | copy-start | bytes 98308
  62.7 3.1 %copy-start = (f32[16,3456]{1,0:T(8,128)S(1)}, f32[16,3456]{1,0:T(8,128)}, u32[]{:S(2)}) copy-start(f32[16,3456]{1,0:T(8,128)} %get-tuple-element.19) | copy-start | bytes 663556
  64.3 0.8 %copy-start.1 = (f32[8,1728]{1,0:T(8,128)S(1)}, f32[8,1728]{1,0:T(8,128)}, u32[]{:S(2)}) copy-start(f32[8,1728]{1,0:T(8,128)} %get-tuple-element.18) | copy-start | bytes 165892

commit v2 on v1

v2 whole, which is shorter than its diff:
```python
import functools
import math

import jax
import jax.numpy as jnp
from jax import lax
from jax.experimental import pallas as pl
from jax.experimental.pallas import tpu as pltpu
from jax.sharding import PartitionSpec as P

MESH = pl.DeviceIdType.MESH
F32 = jnp.float32
BF16 = jnp.bfloat16
PLANE = 256
OWN = 4
SLAB = OWN * PLANE
WIDE1 = SLAB + 2 * PLANE
WIDE2 = SLAB + 4 * PLANE


def at(start, size, unit):
    return pl.ds(pl.multiple_of(start, unit), size)


def plane_at(index, planes=1):
    return at(index * PLANE, planes * PLANE, PLANE)


def place(rows, lanes):
    return lax.broadcasted_iota(jnp.int32, (rows, lanes), 1)


def shifted_x(value, step):
    rows, lanes = value.shape
    x = place(rows, lanes) % 16
    if step > 0:
        return jnp.where(x < 15, pltpu.roll(value, lanes - 1, 1), 0.0)
    return jnp.where(x > 0, pltpu.roll(value, 1, 1), 0.0)


def shifted_y(value, step):
    rows, lanes = value.shape
    cell = place(rows, lanes)
    if step > 0:
        return jnp.where(cell < PLANE - 16, pltpu.roll(value, lanes - 16, 1), 0.0)
    return jnp.where(cell >= 16, pltpu.roll(value, 16, 1), 0.0)


def sigmoid(v):
    return 1.0 / (1.0 + jnp.exp(-v))


def slope(v):
    s = sigmoid(v)
    return s * (1.0 + v * (1.0 - s))


def mm(a, b, ca, cb):
    return lax.dot_general(a, b, (((ca,), (cb,)), ((), ())), preferred_element_type=F32)


def conv_plane(y_ref, rows, p):
    sums = []
    for dy in range(3):
        total = None
        for dz in range(3):
            k = 3 * dz + dy
            part = y_ref[rows * k : rows * (k + 1), plane_at(p + dz)]
            total = part if total is None else total + part
        sums.append(total)
    return sums[1] + shifted_y(sums[0], -1) + shifted_y(sums[2], 1)


def kernel(
    scale, vol, w1, w2, cot, feat, ig_out, g1_out, gq,
    vrecv, wb1, wb2, cb, w1s, w2s, vf, v3, y1, pre1, h, h3, y2, fb, fr, e2,
    ghb, ghr, ghe, e1, igb, igr, gsf, gsx, gsr, gp, gpr, g1f, g1x, g1r, g1t, g1b, g1q,
    loc, vs, vr, w1ss, w1sr, w2ss, w2sr, cs, cr, hs, hr, fs, frs, gs, gr, es, er, xs, xr,
    is_, ir, x1s, x1r, ps, pr, qs, qr, g1s, g1rr,
):
    s = lax.axis_index("sample")
    m = lax.axis_index("mp")
    col = m // 4
    q = m % 4
    waits = []

    def send(src, dst, ssem, rsem, sample, mp):
        c = pltpu.make_async_remote_copy(
            src_ref=src, dst_ref=dst, send_sem=ssem, recv_sem=rsem,
            device_id=(sample, mp), device_id_type=MESH,
        )
        c.start()
        waits.append(c)
        return c

    def slab_peer(r):
        return col * 4 + (q + r) % 4

    def col_peer(r):
        return ((col + r) % 4) * 4 + q

    def to_slabs(source, dst, ssem, rsem):
        return [
            send(source((q + r) % 4, r), dst(r), ssem.at[r - 1], rsem.at[r - 1], s, slab_peer(r))
            for r in (2, 1, 3)
        ]

    barrier = pltpu.get_barrier_semaphore()
    for r in range(1, 16):
        pl.semaphore_signal(barrier, inc=1, device_id=(s, (m + r) % 16), device_id_type=MESH)
    for r in range(1, 8):
        pl.semaphore_signal(barrier, inc=1, device_id=((s + r) % 8, m), device_id_type=MESH)

    def vol_part(slab):
        first = jnp.clip(slab * OWN - 2, 0, 8)
        return vol.at[:, plane_at(first, OWN + 4)]

    def slab_at(slab):
        return at(slab * SLAB, SLAB, SLAB)

    local = [
        pltpu.make_async_copy(vol_part(q), vrecv.at[m], loc.at[0]),
        pltpu.make_async_copy(w1, wb1.at[q], loc.at[1]),
        pltpu.make_async_copy(w2, wb2.at[q], loc.at[2]),
        pltpu.make_async_copy(cot.at[:, slab_at(q)], cb.at[q], loc.at[3]),
    ]
    for c in local:
        c.start()
    gp[27:32] = jnp.zeros((5, 16, 128), BF16)
    vf[...] = jnp.zeros(vf.shape, F32)
    pl.semaphore_wait(barrier, 22)

    vol_copies = []
    for r in (10, 8, 11, 9, 6, 14, 2, 7, 5, 15, 13, 4, 12, 3, 1):
        to = (m + r) % 16
        vol_copies.append(send(vol_part(to % 4), vrecv.at[m], vs.at[r - 1], vr.at[r - 1], s, to))
    w1_copies = to_slabs(lambda slab, r: w1, lambda r: wb1.at[q], w1ss, w1sr)

    local[1].wait()
    for c in w1_copies:
        c.wait_recv()
    w1_all = jnp.concatenate([wb1[i].astype(F32) for i in range(4)], axis=0)
    for k in range(9):
        w1s[32 * k : 32 * k + 32, :] = w1_all[:, 192 * k : 192 * k + 192].astype(BF16)
    local[0].wait()
    for c in vol_copies:
        c.wait_recv()
    core_peer = col * 4 + q + 1 - 2 * (q % 2)
    w2_core = send(w2, wb2.at[q], w2ss.at[0], w2sr.at[0], s, core_peer)
    w2_far = send(w2, wb2.at[q], w2ss.at[1], w2sr.at[1], s, slab_peer(2))
    cot_copies = to_slabs(lambda slab, r: cot.at[:, slab_at(slab)], lambda r: cb.at[q], cs, cr)
    first = jnp.clip(q * OWN - 2, 0, 8) - q * OWN + 4
    for i in range(16):
        vf[4 * i : 4 * i + 4, plane_at(first, OWN + 4)] = vrecv[i].astype(F32)

    for p in range(8):
        lanes = slice(PLANE * p, PLANE * (p + 1))
        value = vf[:, PLANE * (p + 2) : PLANE * (p + 3)]
        for dx in range(3):
            part = value if dx == 1 else shifted_x(value, dx - 1)
            v3[64 * dx : 64 * dx + 64, lanes] = part.astype(BF16)
        y1[:, lanes] = mm(w1s[...], v3[:, lanes], 1, 0)

    rows32 = at(col * 32, 32, 32)
    h_copies = []
    for half in range(2):
        for p in range(3 * half, 3 * half + 3):
            lanes = slice(PLANE * p, PLANE * (p + 1))
            value = conv_plane(y1, 32, p)
            pre1[:, lanes] = value
            z = q * OWN + p - 1
            inside = jnp.logical_and(z >= 0, z < 16)
            hidden = jnp.where(inside, value * sigmoid(value), 0.0)
            h[rows32, lanes] = hidden.astype(BF16)
        part = h.at[rows32, 3 * half * PLANE : 3 * (half + 1) * PLANE]
        for r in (2, 1, 3):
            i = 3 * half + r - 1
            h_copies.append(send(part, part, hs.at[i], hr.at[i], s, col_peer(r)))

    far = wb2.at[(q + 2) % 4]
    w2_far.wait_recv()
    w2_pass = send(far, far, w2ss.at[2], w2sr.at[2], s, core_peer)
    local[2].wait()
    w2_core.wait_recv()
    w2_pass.wait_recv()
    for k in range(9):
        for c in range(4):
            w2s[64 * k + 16 * c : 64 * k + 16 * c + 16, :] = wb2[c, :, 384 * k : 384 * k + 384]
    for half in range(2):
        for c in h_copies[3 * half : 3 * half + 3]:
            c.wait_recv()
        for p in range(3 * half, 3 * half + 3):
            lanes = slice(PLANE * p, PLANE * (p + 1))
            value = h[:, lanes].astype(F32)
            for dx in range(3):
                part = value if dx == 1 else shifted_x(value, dx - 1)
                h3[128 * dx : 128 * dx + 128, lanes] = part.astype(BF16)
            y2[:, lanes] = mm(w2s[...], h3[:, lanes], 1, 0)

    def spread(value, dst, rows, p):
        lanes = slice(PLANE * p, PLANE * (p + 1))
        value = value.astype(BF16).astype(F32)
        dst[0:rows, lanes] = shifted_y(value, 1).astype(BF16)
        dst[rows : 2 * rows, lanes] = value.astype(BF16)
        dst[2 * rows : 3 * rows, lanes] = shifted_y(value, -1).astype(BF16)

    def transposed(w, e, i, rows):
        taps = [dz for dz in range(3) if 0 <= i - dz < OWN]
        parts = [e[:, PLANE * (i - dz) : PLANE * (i - dz + 1)] for dz in taps]
        size = e.shape[0]
        z = mm(w[size * taps[0] : size * (taps[-1] + 1), :], jnp.concatenate(parts, axis=0), 0, 0)
        return z[rows : 2 * rows] + shifted_x(z[:rows], 1) + shifted_x(z[2 * rows :], -1)

    local[3].wait()
    for c in cot_copies:
        c.wait_recv()
    for p in range(OWN):
        lanes = slice(PLANE * p, PLANE * (p + 1))
        value = conv_plane(y2, 64, p)
        sg = sigmoid(value)
        out = (value * sg).astype(BF16)
        for i in range(4):
            fb[i, :, lanes] = out[16 * i : 16 * i + 16]
        cots = jnp.concatenate([cb[i, :, lanes] for i in range(4)], axis=0)
        spread(cots.astype(F32) * (sg * (1.0 + value * (1.0 - sg))), e2, 64, p)

    edge_copies = []
    for side, i in enumerate((0, OWN + 1)):
        lanes = slice(PLANE * i, PLANE * (i + 1))
        ghb[:, lanes] = transposed(w2s, e2, i, 128).astype(BF16)
        for r in (2, 1, 3, 0):
            to = (col + r) % 4
            n = 4 * side + r
            src = ghb.at[at(to * 32, 32, 32), lanes]
            there = to * 4 + (q + 3 - 2 * side) % 4
            edge_copies.append(send(src, ghe.at[n], es.at[n], er.at[n], s, there))
    gh_copies = []
    for half in range(2):
        for i in (1 + 2 * half, 2 + 2 * half):
            lanes = slice(PLANE * i, PLANE * (i + 1))
            ghb[:, lanes] = transposed(w2s, e2, i, 128).astype(BF16)
        lanes = slice(PLANE * (1 + 2 * half), PLANE * (3 + 2 * half))
        for r in (2, 1, 3):
            to = (col + r) % 4
            n = 3 * half + r - 1
            src = ghb.at[at(to * 32, 32, 32), lanes]
            gh_copies.append(send(src, ghr.at[n], gs.at[n], gr.at[n], s, col_peer(r)))

    for dz in range(3):
        part = mm(e2[...], h3[:, PLANE * dz : PLANE * dz + SLAB], 1, 1)
        for dy in range(3):
            gsf[3 * dz + dy] = part[64 * dy : 64 * dy + 64]
    for r in range(1, 4):
        gsx[r - 1] = gsf[:, at(((q + r) % 4) * 16, 16, 16), :].astype(BF16)
    gs_copies = to_slabs(lambda slab, r: gsx.at[r - 1], lambda r: gsr.at[r - 1], xs, xr)
    feat_copies = to_slabs(lambda slab, r: fb.at[slab], lambda r: fr.at[q], fs, frs)

    for c in gh_copies + edge_copies:
        c.wait_recv()
    for p in range(OWN):
        lanes = slice(PLANE * (p + 1), PLANE * (p + 2))
        total = ghb[rows32, lanes].astype(F32)
        part = slice(PLANE * (p % 2), PLANE * (p % 2 + 1))
        for r in range(3):
            total += ghr[3 * (p // 2) + r, :, part].astype(F32)
        for edge, side, inside in ((0, 1, q > 0), (OWN - 1, 0, q < 3)):
            if p == edge:
                more = ghe[4 * side].astype(F32)
                for r in range(1, 4):
                    more += ghe[4 * side + r].astype(F32)
                total += jnp.where(inside, more, 0.0)
        spread(total * slope(pre1[:, lanes]), e1, 32, p)

    for dz in range(3):
        part = mm(e1[...], v3[:, PLANE * (1 + dz) : PLANE * (1 + dz) + SLAB], 1, 1)
        for dy in range(3):
            g1f[3 * dz + dy] = part[32 * dy : 32 * dy + 32]
    for r in range(1, 4):
        g1x[r - 1] = g1f[:, at(((q + r) % 4) * 8, 8, 8), :].astype(BF16)
    g1_copies = to_slabs(lambda slab, r: g1x.at[r - 1], lambda r: g1r.at[r - 1], x1s, x1r)

    for p in range(OWN + 2):
        value = transposed(w1s, e1, p, 64)
        for i in range(16):
            igb[i, :, PLANE * p : PLANE * (p + 1)] = value[4 * i : 4 * i + 4].astype(BF16)
    ig_copies = []
    for r in (10, 8, 11, 9, 6, 14, 2, 7, 5, 15, 13, 4, 12, 3, 1):
        to = (m + r) % 16
        ig_copies.append(send(igb.at[to], igr.at[m], is_.at[r - 1], ir.at[r - 1], s, to))

    for c in gs_copies:
        c.wait_recv()
    mine16 = at(q * 16, 16, 16)
    for k in range(9):
        part = gsf[k, mine16, :]
        for r in range(3):
            part += gsr[r, k].astype(F32)
        part = part.astype(BF16)
        for dx in range(3):
            gp[3 * k + dx] = part[:, 128 * dx : 128 * dx + 128]

    gp_copies = []
    for r in range(1, 8):
        to = (s + r) % 8
        src = gp.at[pl.ds(4 * to, 4)]
        gp_copies.append(send(src, gpr.at[r - 1], ps.at[r - 1], pr.at[r - 1], to, m))

    for c in g1_copies:
        c.wait_recv()
    mine8 = at(q * 8, 8, 8)
    for k in range(9):
        part = g1f[k, mine8, :]
        for r in range(3):
            part += g1r[r, k].astype(F32)
        g1t[:, 192 * k : 192 * k + 192] = part
    g1b[...] = g1t[...].astype(BF16)
    total_copies = []
    for r in range(1, 8):
        to = (s + r) % 8
        total_copies.append(send(g1b, g1q.at[r - 1], g1s.at[r - 1], g1rr.at[r - 1], to, m))

    for c in feat_copies:
        c.wait_recv()
    fr[q] = fb[q]
    for i in range(4):
        feat[:, SLAB * i : SLAB * (i + 1)] = fr[i]
    for c in gp_copies:
        c.wait_recv()
    quarter = pl.ds(4 * s, 4)
    total = gp[quarter].astype(F32)
    for r in range(7):
        total += gpr[r].astype(F32)
    gq[quarter] = (total * scale).astype(BF16)
    gq_copies = []
    for r in range(1, 8):
        to = (s + r) % 8
        gq_copies.append(send(gq.at[quarter], gq.at[quarter], qs.at[r - 1], qr.at[r - 1], to, m))

    igr[m] = igb[m]
    for c in ig_copies:
        c.wait_recv()
    slabs = []
    for i in range(4):
        total = igr[i].astype(F32)
        for x in range(1, 4):
            total += igr[4 * x + i].astype(F32)
        slabs.append(total)
    for z in range(16):
        i, p = z // OWN, z % OWN
        total = slabs[i][:, PLANE * (p + 1) : PLANE * (p + 2)]
        if p == OWN - 1 and i < 3:
            total += slabs[i + 1][:, :PLANE]
        if p == 0 and i > 0:
            total += slabs[i - 1][:, PLANE * (OWN + 1) :]
        ig_out[:, PLANE * z : PLANE * (z + 1)] = total.astype(BF16)

    for c in total_copies:
        c.wait_recv()
    total = g1t[...]
    for r in range(7):
        total += g1q[r].astype(F32)
    g1_out[...] = total * scale

    for c in gq_copies:
        c.wait_recv()

    for c in waits:
        c.wait_send()


def finish(feat, ig, g1, gq, feat_out, ig_out, g1_out, g2_out):
    feat_out[...] = feat[...]
    ig_out[...] = ig[...]
    g1_out[...] = g1[...]
    for t in range(27):
        g2_out[:, 128 * t : 128 * t + 128] = gq[t].astype(F32)


def local_step(volumes, w_first, w_second, cotangent):
    cells = 4 * SLAB
    scale = 1.0 / math.sqrt(lax.axis_size("sample") * volumes.shape[1] * cells)
    V = pltpu.VMEM
    dma = pltpu.SemaphoreType.DMA
    scratch = [
        V((16, 4, WIDE2), BF16), V((4, 8, 1728), BF16), V((4, 16, 3456), BF16), V((4, 16, SLAB), BF16),
        V((288, 192), BF16), V((576, 384), BF16), V((64, 12 * PLANE), F32), V((192, WIDE2), BF16),
        V((288, WIDE2), F32), V((32, WIDE1), F32), V((128, WIDE1), BF16), V((384, WIDE1), BF16),
        V((576, WIDE1), F32), V((4, 16, SLAB), BF16), V((4, 16, SLAB), BF16), V((192, SLAB), BF16),
        V((128, WIDE1), BF16), V((6, 32, 2 * PLANE), BF16), V((8, 32, PLANE), BF16),
        V((96, SLAB), BF16), V((16, 4, WIDE1), BF16), V((16, 4, WIDE1), BF16),
        V((9, 64, 384), F32), V((3, 9, 16, 384), BF16), V((3, 9, 16, 384), BF16),
        V((32, 16, 128), BF16), V((7, 4, 16, 128), BF16),
        V((9, 32, 192), F32), V((3, 9, 8, 192), BF16), V((3, 9, 8, 192), BF16),
        V((8, 1728), F32), V((8, 1728), BF16), V((7, 8, 1728), BF16),
    ] + [
        dma((n,)) for n in
        (4, 15, 15, 3, 3, 3, 3, 3, 3, 6, 6, 3, 3, 6, 6, 8, 8, 3, 3, 15, 15, 3, 3, 7, 7, 7, 7, 7, 7)
    ]
    hbm = pl.BlockSpec(memory_space=pltpu.HBM)
    vmem = pl.BlockSpec(memory_space=pltpu.VMEM)
    parts = pl.pallas_call(
        functools.partial(kernel, scale),
        out_shape=(
            jax.ShapeDtypeStruct((16, cells), BF16),
            jax.ShapeDtypeStruct((4, cells), BF16),
            jax.ShapeDtypeStruct((8, 1728), F32),
            jax.ShapeDtypeStruct((32, 16, 128), BF16),
        ),
        in_specs=[hbm] * 4,
        out_specs=(vmem,) * 4,
        scratch_shapes=scratch,
        compiler_params=pltpu.CompilerParams(
            collective_id=0, has_side_effects=True, vmem_limit_bytes=48 * 1024 * 1024
        ),
    )(volumes.reshape(4, cells), w_first, w_second, cotangent.reshape(16, cells))
    feat, ig, g1, g2 = pl.pallas_call(
        finish,
        out_shape=(
            jax.ShapeDtypeStruct((16, cells), BF16),
            jax.ShapeDtypeStruct((4, cells), BF16),
            jax.ShapeDtypeStruct((8, 1728), F32),
            jax.ShapeDtypeStruct((16, 3456), F32),
        ),
        in_specs=[vmem] * 4,
        out_specs=(vmem,) * 4,
        compiler_params=pltpu.CompilerParams(vmem_limit_bytes=8 * 1024 * 1024),
    )(*parts)
    return feat.reshape(16, 1, cells), ig.reshape(4, 1, cells), g1, g2


def solution(mesh):
    return jax.shard_map(
        local_step,
        mesh=mesh,
        in_specs=(P("mp", "sample", None), P("mp", None), P("mp", None), P("mp", "sample", None)),
        out_specs=(P("mp", "sample", None), P("mp", "sample", None), P("mp", None), P("mp", None)),
        check_vma=False,
    )
```

time: 66.6 us -> 52.9 us (0.79)
  Pallas kernels: 62 us -> 48.7 us
    pallas_call x1, Pallas kernels: 62 us -> 47.9 us  [local_step(): pl.pallas_call(functools.partial(kernel, scale), out_shape=(jax.ShapeDtyp...]
    pallas_call x0 -> x1, Pallas kernels: none -> 0.76 us  [local_step(): pl.pallas_call(finish, out_shape=(jax.ShapeDtypeStruct((16, cells), BF16)...]
    unnamed x10 -> x8, local copies, waits for them, and re-layouts: 3.76 us -> 3.3 us
where the time goes in v2:
time: 52.9 us; the launch traced here: 52.6 us
  Pallas kernels  48.7 us (92%)
  local copies, waits for them, and re-layouts  3.3 us (6%)
  between operations  0.65 us (1%)
    pallas_call x1, Pallas kernels, local_step(): pl.pallas_call(functools.partial(kernel, scale), out_shape=(jax.ShapeDtyp...  47.9 us
    unnamed x8, local copies, waits for them, and re-layouts  3.3 us

profile of v2, /device:TPU:1, one launch (start us, length us, event | category | flops | bytes accessed | tf_op | source)
XLA Modules:
  0.0 52.6 jit_solution(58706100779868423)
XLA Ops:
  0.6 0.0 copy-start
  0.6 0.9 %copy-done = bf16[16,1,4096]{2,0,1:T(8,128)(2,1)S(1)} copy-done((bf16[16,1,4096]{2,0,1:T(8,128)(2,1)S(1)}, bf16[16,1,4096]{2,0,1:T(8,128)(2,1)}, u32[]{:S(2)}) %copy-start) | copy-done | bytes 131096
  1.5 0.0 copy-start.1
  1.5 0.9 %copy-done.1 = bf16[16,3456]{1,0:T(8,128)(2,1)S(1)} copy-done((bf16[16,3456]{1,0:T(8,128)(2,1)S(1)}, bf16[16,3456]{1,0:T(8,128)(2,1)}, u32[]{:S(2)}) %copy-start.1) | copy-done | bytes 110616
  2.4 0.0 copy-start.2
  2.4 0.8 %copy-done.2 = bf16[4,1,4096]{2,0,1:T(4,128)(2,1)S(1)} copy-done((bf16[4,1,4096]{2,0,1:T(4,128)(2,1)S(1)}, bf16[4,1,4096]{2,0,1:T(4,128)(2,1)}, u32[]{:S(2)}) %copy-start.2) | copy-done | bytes 32792
  3.2 0.0 copy-start.3
  3.2 0.7 %copy-done.3 = bf16[8,1728]{1,0:T(8,128)(2,1)S(1)} copy-done((bf16[8,1728]{1,0:T(8,128)(2,1)S(1)}, bf16[8,1728]{1,0:T(8,128)(2,1)}, u32[]{:S(2)}) %copy-start.3) | copy-done | bytes 27672
  3.9 47.9 %shard_map.75 = (bf16[16,4096]{1,0:T(8,128)(2,1)S(1)}, bf16[4,4096]{1,0:T(4,128)(2,1)S(1)}, f32[8,1728]{1,0:T(8,128)S(1)}, bf16[32,16,128]{2,1,0:T(8,128)(2,1)S(1)}) custom-call(bf16[4,4096]{1,0:T(4,128)(2,1)S(1)} %bitcast.5, bf16[8,1728]{1,0:T(8,128)(2,1)S(1)} %copy-done.3, bf16[16,3456]{1,0:T(8,128)(2,1)S(1)} %copy-done.1, bf16[16,4096]{1,0:T(8,128)(2,1)S(1)} %bitcast.4), custom_call_target="tpu_custom_call" | custom-call | tf_op jit(solution)/shard_map/pallas_call | solution.py:401
  51.9 0.8 %shard_map.76 = (bf16[16,4096]{1,0:T(8,128)(2,1)}, bf16[4,4096]{1,0:T(4,128)(2,1)}, f32[8,1728]{1,0:T(8,128)}, f32[16,3456]{1,0:T(8,128)}) custom-call(bf16[16,4096]{1,0:T(8,128)(2,1)S(1)} %get-tuple-element.12.feat, bf16[4,4096]{1,0:T(4,128)(2,1)S(1)} %get-tuple-element.13.ig, f32[8,1728]{1,0:T(8,128)S(1)} %get-tuple-element.14.g1, ...), custom_call_target="tpu_custom_call" | custom-call | tf_op jit(solution)/shard_map/pallas_call | solution.py:416
Async XLA Ops:
  0.6 0.9 %copy-start = (bf16[16,1,4096]{2,0,1:T(8,128)(2,1)S(1)}, bf16[16,1,4096]{2,0,1:T(8,128)(2,1)}, u32[]{:S(2)}) copy-start(bf16[16,1,4096]{2,0,1:T(8,128)(2,1)} %param.7) | copy-start | bytes 393220
  1.5 0.9 %copy-start.1 = (bf16[16,3456]{1,0:T(8,128)(2,1)S(1)}, bf16[16,3456]{1,0:T(8,128)(2,1)}, u32[]{:S(2)}) copy-start(bf16[16,3456]{1,0:T(8,128)(2,1)} %w2.1) | copy-start | bytes 331780
  2.4 0.8 %copy-start.2 = (bf16[4,1,4096]{2,0,1:T(4,128)(2,1)S(1)}, bf16[4,1,4096]{2,0,1:T(4,128)(2,1)}, u32[]{:S(2)}) copy-start(bf16[4,1,4096]{2,0,1:T(4,128)(2,1)} %param.4) | copy-start | bytes 98308
  3.2 0.7 %copy-start.3 = (bf16[8,1728]{1,0:T(8,128)(2,1)S(1)}, bf16[8,1728]{1,0:T(8,128)(2,1)}, u32[]{:S(2)}) copy-start(bf16[8,1728]{1,0:T(8,128)(2,1)} %w1.1) | copy-start | bytes 82948

commit v3 on v2

--- a/solution.py
+++ b/solution.py
@@ -250,10 +250,13 @@
         part = mm(e2[...], h3[:, PLANE * dz : PLANE * dz + SLAB], 1, 1)
         for dy in range(3):
             gsf[3 * dz + dy] = part[64 * dy : 64 * dy + 64]
-    for r in range(1, 4):
-        gsx[r - 1] = gsf[:, at(((q + r) % 4) * 16, 16, 16), :].astype(BF16)
-    gs_copies = to_slabs(lambda slab, r: gsx.at[r - 1], lambda r: gsr.at[r - 1], xs, xr)
-    feat_copies = to_slabs(lambda slab, r: fb.at[slab], lambda r: fr.at[q], fs, frs)
+    core, pair = q % 2, q // 2
+    for i in range(2):
+        gsx[i] = gsf[:, at((2 * i + 1 - core) * 16, 16, 16), :].astype(BF16)
+    core_copy = send(gsx.at[0:2], gsr.at[0:2], xs.at[0], xr.at[0], s, core_peer)
+    core_copy.wait_recv()
+    gsx[2] = (gsf[:, at((2 * (1 - pair) + core) * 16, 16, 16), :] + gsr[1 - pair].astype(F32)).astype(BF16)
+    pair_copy = send(gsx.at[2], gsr.at[2], xs.at[1], xr.at[1], s, slab_peer(2))
 
     for c in gh_copies + edge_copies:
         c.wait_recv()
@@ -288,17 +291,12 @@
         to = (m + r) % 16
         ig_copies.append(send(igb.at[to], igr.at[m], is_.at[r - 1], ir.at[r - 1], s, to))
 
-    for c in gs_copies:
-        c.wait_recv()
-    mine16 = at(q * 16, 16, 16)
+    pair_copy.wait_recv()
     for k in range(9):
-        part = gsf[k, mine16, :]
-        for r in range(3):
-            part += gsr[r, k].astype(F32)
+        part = gsf[k, at(q * 16, 16, 16), :] + gsr[pair, k].astype(F32) + gsr[2, k].astype(F32)
         part = part.astype(BF16)
         for dx in range(3):
             gp[3 * k + dx] = part[:, 128 * dx : 128 * dx + 128]
-
     gp_copies = []
     for r in range(1, 8):
         to = (s + r) % 8
@@ -318,12 +316,8 @@
     for r in range(1, 8):
         to = (s + r) % 8
         total_copies.append(send(g1b, g1q.at[r - 1], g1s.at[r - 1], g1rr.at[r - 1], to, m))
-
-    for c in feat_copies:
-        c.wait_recv()
-    fr[q] = fb[q]
-    for i in range(4):
-        feat[:, SLAB * i : SLAB * (i + 1)] = fr[i]
+    feat_copies = to_slabs(lambda slab, r: fb.at[slab], lambda r: fr.at[q], fs, frs)
+
     for c in gp_copies:
         c.wait_recv()
     quarter = pl.ds(4 * s, 4)
@@ -336,6 +330,11 @@
         to = (s + r) % 8
         gq_copies.append(send(gq.at[quarter], gq.at[quarter], qs.at[r - 1], qr.at[r - 1], to, m))
 
+    for c in feat_copies:
+        c.wait_recv()
+    fr[q] = fb[q]
+    for i in range(4):
+        feat[:, SLAB * i : SLAB * (i + 1)] = fr[i]
     igr[m] = igb[m]
     for c in ig_copies:
         c.wait_recv()
@@ -397,6 +396,8 @@
         (4, 15, 15, 3, 3, 3, 3, 3, 3, 6, 6, 3, 3, 6, 6, 8, 8, 3, 3, 15, 15, 3, 3, 7, 7, 7, 7, 7, 7)
     ]
     hbm = pl.BlockSpec(memory_space=pltpu.HBM)
+    given = (volumes.reshape(4, cells), w_first, w_second, cotangent.reshape(16, cells))
+    given = [pltpu.with_memory_space_constraint(a, pltpu.HBM) for a in given]
     vmem = pl.BlockSpec(memory_space=pltpu.VMEM)
     parts = pl.pallas_call(
         functools.partial(kernel, scale),
@@ -412,7 +413,7 @@
         compiler_params=pltpu.CompilerParams(
             collective_id=0, has_side_effects=True, vmem_limit_bytes=48 * 1024 * 1024
         ),
-    )(volumes.reshape(4, cells), w_first, w_second, cotangent.reshape(16, cells))
+    )(*given)
     feat, ig, g1, g2 = pl.pallas_call(
         finish,
         out_shape=(

time: 52.9 us -> 48.5 us (0.917)
  local copies, waits for them, and re-layouts: 3.3 us -> 0 us
  Pallas kernels: 48.7 us -> 47.7 us
    unnamed x8 -> x0, local copies, waits for them, and re-layouts: 3.3 us -> none
    pallas_call x1, Pallas kernels: 47.9 us -> 46.9 us  [local_step(): pl.pallas_call(functools.partial(kernel, scale), out_shape=(jax.ShapeDtyp...]
where the time goes in v3:
time: 48.5 us; the launch traced here: 48.3 us
  Pallas kernels  47.7 us (98%)
  between operations  0.64 us (1%)
    pallas_call x1, Pallas kernels, local_step(): pl.pallas_call(functools.partial(kernel, scale), out_shape=(jax.ShapeDtyp...  46.9 us

profile of v3, /device:TPU:1, one launch (start us, length us, event | category | flops | bytes accessed | tf_op | source)
XLA Modules:
  0.0 48.3 jit_solution(7130303071114689389)
XLA Ops:
  0.6 46.9 %shard_map.75 = (bf16[16,4096]{1,0:T(8,128)(2,1)S(1)}, bf16[4,4096]{1,0:T(4,128)(2,1)S(1)}, f32[8,1728]{1,0:T(8,128)S(1)}, bf16[32,16,128]{2,1,0:T(8,128)(2,1)S(1)}) custom-call(bf16[4,4096]{1,0:T(4,128)(2,1)} %bitcast.5, bf16[8,1728]{1,0:T(8,128)(2,1)} %w1.1, bf16[16,3456]{1,0:T(8,128)(2,1)} %w2.1, bf16[16,4096]{1,0:T(8,128)(2,1)} %bitcast.4), custom_call_target="tpu_custom_call" | custom-call | tf_op jit(solution)/shard_map/pallas_call | solution.py:402
  47.6 0.8 %shard_map.76 = (bf16[16,4096]{1,0:T(8,128)(2,1)}, bf16[4,4096]{1,0:T(4,128)(2,1)}, f32[8,1728]{1,0:T(8,128)}, f32[16,3456]{1,0:T(8,128)}) custom-call(bf16[16,4096]{1,0:T(8,128)(2,1)S(1)} %get-tuple-element.12.feat, bf16[4,4096]{1,0:T(4,128)(2,1)S(1)} %get-tuple-element.13.ig, f32[8,1728]{1,0:T(8,128)S(1)} %get-tuple-element.14.g1, ...), custom_call_target="tpu_custom_call" | custom-call | tf_op jit(solution)/shard_map/pallas_call | solution.py:417

commit v4 on v3

--- a/solution.py
+++ b/solution.py
@@ -14,6 +14,7 @@
 PLANE = 256
 OWN = 4
 SLAB = OWN * PLANE
+CHUNK = 2
 WIDE1 = SLAB + 2 * PLANE
 WIDE2 = SLAB + 4 * PLANE
 
@@ -110,6 +111,12 @@
         pl.semaphore_signal(barrier, inc=1, device_id=(s, (m + r) % 16), device_id_type=MESH)
     for r in range(1, 8):
         pl.semaphore_signal(barrier, inc=1, device_id=((s + r) % 8, m), device_id_type=MESH)
+    for r in range(1, 8):
+        there = ((s + r) % 8, col * 4 + (q + 2) % 4)
+        pl.semaphore_signal(barrier, inc=1, device_id=there, device_id_type=MESH)
+    for r in (1, 3):
+        there = ((s + 4) % 8, col * 4 + (q + r) % 4)
+        pl.semaphore_signal(barrier, inc=1, device_id=there, device_id_type=MESH)
 
     def vol_part(slab):
         first = jnp.clip(slab * OWN - 2, 0, 8)
@@ -126,15 +133,18 @@
     ]
     for c in local:
         c.start()
-    gp[27:32] = jnp.zeros((5, 16, 128), BF16)
+    gp[:, 27:32] = jnp.zeros((2, 5, 16, 128), BF16)
     vf[...] = jnp.zeros(vf.shape, F32)
-    pl.semaphore_wait(barrier, 22)
+    pl.semaphore_wait(barrier, 31)
 
     vol_copies = []
     for r in (10, 8, 11, 9, 6, 14, 2, 7, 5, 15, 13, 4, 12, 3, 1):
         to = (m + r) % 16
         vol_copies.append(send(vol_part(to % 4), vrecv.at[m], vs.at[r - 1], vr.at[r - 1], s, to))
     w1_copies = to_slabs(lambda slab, r: w1, lambda r: wb1.at[q], w1ss, w1sr)
+    core_peer = col * 4 + q + 1 - 2 * (q % 2)
+    w2_core = send(w2, wb2.at[q], w2ss.at[0], w2sr.at[0], s, core_peer)
+    w2_far = send(w2, wb2.at[q], w2ss.at[1], w2sr.at[1], s, slab_peer(2))
 
     local[1].wait()
     for c in w1_copies:
@@ -145,15 +155,12 @@
     local[0].wait()
     for c in vol_copies:
         c.wait_recv()
-    core_peer = col * 4 + q + 1 - 2 * (q % 2)
-    w2_core = send(w2, wb2.at[q], w2ss.at[0], w2sr.at[0], s, core_peer)
-    w2_far = send(w2, wb2.at[q], w2ss.at[1], w2sr.at[1], s, slab_peer(2))
     cot_copies = to_slabs(lambda slab, r: cot.at[:, slab_at(slab)], lambda r: cb.at[q], cs, cr)
     first = jnp.clip(q * OWN - 2, 0, 8) - q * OWN + 4
     for i in range(16):
         vf[4 * i : 4 * i + 4, plane_at(first, OWN + 4)] = vrecv[i].astype(F32)
 
-    for p in range(8):
+    def products_v(p):
         lanes = slice(PLANE * p, PLANE * (p + 1))
         value = vf[:, PLANE * (p + 2) : PLANE * (p + 3)]
         for dx in range(3):
@@ -163,19 +170,22 @@
 
     rows32 = at(col * 32, 32, 32)
     h_copies = []
-    for half in range(2):
-        for p in range(3 * half, 3 * half + 3):
-            lanes = slice(PLANE * p, PLANE * (p + 1))
-            value = conv_plane(y1, 32, p)
-            pre1[:, lanes] = value
-            z = q * OWN + p - 1
-            inside = jnp.logical_and(z >= 0, z < 16)
-            hidden = jnp.where(inside, value * sigmoid(value), 0.0)
-            h[rows32, lanes] = hidden.astype(BF16)
-        part = h.at[rows32, 3 * half * PLANE : 3 * (half + 1) * PLANE]
-        for r in (2, 1, 3):
-            i = 3 * half + r - 1
-            h_copies.append(send(part, part, hs.at[i], hr.at[i], s, col_peer(r)))
+    products_v(0)
+    products_v(1)
+    for p in range(OWN + 2):
+        products_v(p + 2)
+        lanes = slice(PLANE * p, PLANE * (p + 1))
+        value = conv_plane(y1, 32, p)
+        pre1[:, lanes] = value
+        z = q * OWN + p - 1
+        inside = jnp.logical_and(z >= 0, z < 16)
+        hidden = jnp.where(inside, value * sigmoid(value), 0.0)
+        h[rows32, lanes] = hidden.astype(BF16)
+        if p % CHUNK == CHUNK - 1:
+            part = h.at[rows32, PLANE * (p + 1 - CHUNK) : PLANE * (p + 1)]
+            for r in (2, 1, 3):
+                i = 3 * (p // CHUNK) + r - 1
+                h_copies.append(send(part, part, hs.at[i], hr.at[i], s, col_peer(r)))
 
     far = wb2.at[(q + 2) % 4]
     w2_far.wait_recv()
@@ -186,16 +196,16 @@
     for k in range(9):
         for c in range(4):
             w2s[64 * k + 16 * c : 64 * k + 16 * c + 16, :] = wb2[c, :, 384 * k : 384 * k + 384]
-    for half in range(2):
-        for c in h_copies[3 * half : 3 * half + 3]:
-            c.wait_recv()
-        for p in range(3 * half, 3 * half + 3):
-            lanes = slice(PLANE * p, PLANE * (p + 1))
-            value = h[:, lanes].astype(F32)
-            for dx in range(3):
-                part = value if dx == 1 else shifted_x(value, dx - 1)
-                h3[128 * dx : 128 * dx + 128, lanes] = part.astype(BF16)
-            y2[:, lanes] = mm(w2s[...], h3[:, lanes], 1, 0)
+    for p in range(OWN + 2):
+        if p % CHUNK == 0:
+            for c in h_copies[3 * (p // CHUNK) : 3 * (p // CHUNK) + 3]:
+                c.wait_recv()
+        lanes = slice(PLANE * p, PLANE * (p + 1))
+        value = h[:, lanes].astype(F32)
+        for dx in range(3):
+            part = value if dx == 1 else shifted_x(value, dx - 1)
+            h3[128 * dx : 128 * dx + 128, lanes] = part.astype(BF16)
+        y2[:, lanes] = mm(w2s[...], h3[:, lanes], 1, 0)
 
     def spread(value, dst, rows, p):
         lanes = slice(PLANE * p, PLANE * (p + 1))
@@ -255,8 +265,18 @@
         gsx[i] = gsf[:, at((2 * i + 1 - core) * 16, 16, 16), :].astype(BF16)
     core_copy = send(gsx.at[0:2], gsr.at[0:2], xs.at[0], xr.at[0], s, core_peer)
     core_copy.wait_recv()
-    gsx[2] = (gsf[:, at((2 * (1 - pair) + core) * 16, 16, 16), :] + gsr[1 - pair].astype(F32)).astype(BF16)
-    pair_copy = send(gsx.at[2], gsr.at[2], xs.at[1], xr.at[1], s, slab_peer(2))
+    for i in range(2):
+        mine = at((2 * i + core) * 16, 16, 16)
+        for k in range(9):
+            part = (gsf[k, mine, :] + gsr[i, k].astype(F32)).astype(BF16)
+            for dx in range(3):
+                gp[i, 3 * k + dx] = part[:, 128 * dx : 128 * dx + 128]
+    gp_copies = []
+    for r in (8, 7, 9, 6, 10, 5, 11, 4, 12, 3, 13, 2, 14, 1, 15):
+        to = (s * 2 + pair + r) % 16
+        src = gp.at[to % 2, pl.ds(4 * (to // 2), 4)]
+        there = col * 4 + (to % 2) * 2 + core
+        gp_copies.append(send(src, gpr.at[r - 1], ps.at[r - 1], pr.at[r - 1], to // 2, there))
 
     for c in gh_copies + edge_copies:
         c.wait_recv()
@@ -278,9 +298,14 @@
         part = mm(e1[...], v3[:, PLANE * (1 + dz) : PLANE * (1 + dz) + SLAB], 1, 1)
         for dy in range(3):
             g1f[3 * dz + dy] = part[32 * dy : 32 * dy + 32]
-    for r in range(1, 4):
-        g1x[r - 1] = g1f[:, at(((q + r) % 4) * 8, 8, 8), :].astype(BF16)
-    g1_copies = to_slabs(lambda slab, r: g1x.at[r - 1], lambda r: g1r.at[r - 1], x1s, x1r)
+    for i in range(4):
+        g1x[i] = g1f[:, 8 * i : 8 * i + 8, :].astype(BF16)
+    g1_copies = []
+    for r in (2, 6, 3, 5, 1, 7, 4):
+        to = ((s // 4) * 4 + q + r) % 8
+        there = (to // 4) * 4 + s % 4
+        src = g1x.at[to % 4]
+        g1_copies.append(send(src, g1r.at[r - 1], x1s.at[r - 1], x1r.at[r - 1], there, col * 4 + to % 4))
 
     for p in range(OWN + 2):
         value = transposed(w1s, e1, p, 64)
@@ -291,44 +316,32 @@
         to = (m + r) % 16
         ig_copies.append(send(igb.at[to], igr.at[m], is_.at[r - 1], ir.at[r - 1], s, to))
 
-    pair_copy.wait_recv()
-    for k in range(9):
-        part = gsf[k, at(q * 16, 16, 16), :] + gsr[pair, k].astype(F32) + gsr[2, k].astype(F32)
-        part = part.astype(BF16)
-        for dx in range(3):
-            gp[3 * k + dx] = part[:, 128 * dx : 128 * dx + 128]
-    gp_copies = []
-    for r in range(1, 8):
-        to = (s + r) % 8
-        src = gp.at[pl.ds(4 * to, 4)]
-        gp_copies.append(send(src, gpr.at[r - 1], ps.at[r - 1], pr.at[r - 1], to, m))
-
-    for c in g1_copies:
-        c.wait_recv()
-    mine8 = at(q * 8, 8, 8)
-    for k in range(9):
-        part = g1f[k, mine8, :]
-        for r in range(3):
-            part += g1r[r, k].astype(F32)
-        g1t[:, 192 * k : 192 * k + 192] = part
-    g1b[...] = g1t[...].astype(BF16)
-    total_copies = []
-    for r in range(1, 8):
-        to = (s + r) % 8
-        total_copies.append(send(g1b, g1q.at[r - 1], g1s.at[r - 1], g1rr.at[r - 1], to, m))
-    feat_copies = to_slabs(lambda slab, r: fb.at[slab], lambda r: fr.at[q], fs, frs)
-
     for c in gp_copies:
         c.wait_recv()
     quarter = pl.ds(4 * s, 4)
-    total = gp[quarter].astype(F32)
-    for r in range(7):
+    total = gp[pair, quarter].astype(F32)
+    for r in range(15):
         total += gpr[r].astype(F32)
     gq[quarter] = (total * scale).astype(BF16)
     gq_copies = []
     for r in range(1, 8):
         to = (s + r) % 8
         gq_copies.append(send(gq.at[quarter], gq.at[quarter], qs.at[r - 1], qr.at[r - 1], to, m))
+
+    for c in g1_copies:
+        c.wait_recv()
+    mine8 = at(q * 8, 8, 8)
+    for k in range(9):
+        part = g1f[k, mine8, :]
+        for r in range(7):
+            part += g1r[r, k].astype(F32)
+        g1t[:, 192 * k : 192 * k + 192] = part
+    g1b[...] = g1t[...].astype(BF16)
+    total_copies = []
+    for r in (2, 1, 3):
+        to = (s // 4) * 4 + (s + r) % 4
+        total_copies.append(send(g1b, g1q.at[r - 1], g1s.at[r - 1], g1rr.at[r - 1], to, m))
+    feat_copies = to_slabs(lambda slab, r: fb.at[slab], lambda r: fr.at[q], fs, frs)
 
     for c in feat_copies:
         c.wait_recv()
@@ -356,7 +369,7 @@
     for c in total_copies:
         c.wait_recv()
     total = g1t[...]
-    for r in range(7):
+    for r in range(3):
         total += g1q[r].astype(F32)
     g1_out[...] = total * scale
 
@@ -387,13 +400,13 @@
         V((576, WIDE1), F32), V((4, 16, SLAB), BF16), V((4, 16, SLAB), BF16), V((192, SLAB), BF16),
         V((128, WIDE1), BF16), V((6, 32, 2 * PLANE), BF16), V((8, 32, PLANE), BF16),
         V((96, SLAB), BF16), V((16, 4, WIDE1), BF16), V((16, 4, WIDE1), BF16),
-        V((9, 64, 384), F32), V((3, 9, 16, 384), BF16), V((3, 9, 16, 384), BF16),
-        V((32, 16, 128), BF16), V((7, 4, 16, 128), BF16),
-        V((9, 32, 192), F32), V((3, 9, 8, 192), BF16), V((3, 9, 8, 192), BF16),
-        V((8, 1728), F32), V((8, 1728), BF16), V((7, 8, 1728), BF16),
+        V((9, 64, 384), F32), V((2, 9, 16, 384), BF16), V((2, 9, 16, 384), BF16),
+        V((2, 32, 16, 128), BF16), V((15, 4, 16, 128), BF16),
+        V((9, 32, 192), F32), V((4, 9, 8, 192), BF16), V((7, 9, 8, 192), BF16),
+        V((8, 1728), F32), V((8, 1728), BF16), V((3, 8, 1728), BF16),
     ] + [
         dma((n,)) for n in
-        (4, 15, 15, 3, 3, 3, 3, 3, 3, 6, 6, 3, 3, 6, 6, 8, 8, 3, 3, 15, 15, 3, 3, 7, 7, 7, 7, 7, 7)
+        (4, 15, 15, 3, 3, 3, 3, 3, 3, 18, 18, 3, 3, 6, 6, 8, 8, 3, 3, 15, 15, 7, 7, 15, 15, 7, 7, 3, 3)
     ]
     hbm = pl.BlockSpec(memory_space=pltpu.HBM)
     given = (volumes.reshape(4, cells), w_first, w_second, cotangent.reshape(16, cells))

time: 48.5 us -> 47.2 us (0.973)
  Pallas kernels: 47.7 us -> 46.4 us
    pallas_call x1, Pallas kernels: 46.9 us -> 45.7 us  [local_step(): pl.pallas_call(functools.partial(kernel, scale), out_shape=(jax.ShapeDtyp...]
where the time goes in v4:
time: 47.2 us; the launch traced here: 47.1 us
  Pallas kernels  46.4 us (98%)
  between operations  0.64 us (1%)
    pallas_call x1, Pallas kernels, local_step(): pl.pallas_call(functools.partial(kernel, scale), out_shape=(jax.ShapeDtyp...  45.7 us

profile of v4, /device:TPU:1, one launch (start us, length us, event | category | flops | bytes accessed | tf_op | source)
XLA Modules:
  0.0 47.1 jit_solution(16123783785956451861)
XLA Ops:
  0.6 45.7 %shard_map.75 = (bf16[16,4096]{1,0:T(8,128)(2,1)S(1)}, bf16[4,4096]{1,0:T(4,128)(2,1)S(1)}, f32[8,1728]{1,0:T(8,128)S(1)}, bf16[32,16,128]{2,1,0:T(8,128)(2,1)S(1)}) custom-call(bf16[4,4096]{1,0:T(4,128)(2,1)} %bitcast.5, bf16[8,1728]{1,0:T(8,128)(2,1)} %w1.1, bf16[16,3456]{1,0:T(8,128)(2,1)} %w2.1, bf16[16,4096]{1,0:T(8,128)(2,1)} %bitcast.4), custom_call_target="tpu_custom_call" | custom-call | tf_op jit(solution)/shard_map/pallas_call | solution.py:415
  46.3 0.8 %shard_map.76 = (bf16[16,4096]{1,0:T(8,128)(2,1)}, bf16[4,4096]{1,0:T(4,128)(2,1)}, f32[8,1728]{1,0:T(8,128)}, f32[16,3456]{1,0:T(8,128)}) custom-call(bf16[16,4096]{1,0:T(8,128)(2,1)S(1)} %get-tuple-element.12.feat, bf16[4,4096]{1,0:T(4,128)(2,1)S(1)} %get-tuple-element.13.ig, f32[8,1728]{1,0:T(8,128)S(1)} %get-tuple-element.14.g1, ...), custom_call_target="tpu_custom_call" | custom-call | tf_op jit(solution)/shard_map/pallas_call | solution.py:430

commit v5 on v4

--- a/solution.py
+++ b/solution.py
@@ -14,7 +14,7 @@
 PLANE = 256
 OWN = 4
 SLAB = OWN * PLANE
-CHUNK = 2
+CHUNK = 1
 WIDE1 = SLAB + 2 * PLANE
 WIDE2 = SLAB + 4 * PLANE
 
@@ -137,11 +137,11 @@
     vf[...] = jnp.zeros(vf.shape, F32)
     pl.semaphore_wait(barrier, 31)
 
+    w1_copies = to_slabs(lambda slab, r: w1, lambda r: wb1.at[q], w1ss, w1sr)
     vol_copies = []
     for r in (10, 8, 11, 9, 6, 14, 2, 7, 5, 15, 13, 4, 12, 3, 1):
         to = (m + r) % 16
         vol_copies.append(send(vol_part(to % 4), vrecv.at[m], vs.at[r - 1], vr.at[r - 1], s, to))
-    w1_copies = to_slabs(lambda slab, r: w1, lambda r: wb1.at[q], w1ss, w1sr)
     core_peer = col * 4 + q + 1 - 2 * (q % 2)
     w2_core = send(w2, wb2.at[q], w2ss.at[0], w2sr.at[0], s, core_peer)
     w2_far = send(w2, wb2.at[q], w2ss.at[1], w2sr.at[1], s, slab_peer(2))

time: 47.2 us -> 46.5 us (0.985)
  Pallas kernels: 46.4 us -> 45.7 us
    pallas_call x1, Pallas kernels: 45.7 us -> 45 us  [local_step(): pl.pallas_call(functools.partial(kernel, scale), out_shape=(jax.ShapeDtyp...]
where the time goes in v5:
time: 46.5 us; the launch traced here: 46.4 us
  Pallas kernels  45.7 us (98%)
  between operations  0.64 us (1%)
    pallas_call x1, Pallas kernels, local_step(): pl.pallas_call(functools.partial(kernel, scale), out_shape=(jax.ShapeDtyp...  45 us

profile of v5, /device:TPU:1, one launch (start us, length us, event | category | flops | bytes accessed | tf_op | source)
XLA Modules:
  0.0 46.4 jit_solution(15571834241084703989)
XLA Ops:
  0.6 45.0 %shard_map.75 = (bf16[16,4096]{1,0:T(8,128)(2,1)S(1)}, bf16[4,4096]{1,0:T(4,128)(2,1)S(1)}, f32[8,1728]{1,0:T(8,128)S(1)}, bf16[32,16,128]{2,1,0:T(8,128)(2,1)S(1)}) custom-call(bf16[4,4096]{1,0:T(4,128)(2,1)} %bitcast.5, bf16[8,1728]{1,0:T(8,128)(2,1)} %w1.1, bf16[16,3456]{1,0:T(8,128)(2,1)} %w2.1, bf16[16,4096]{1,0:T(8,128)(2,1)} %bitcast.4), custom_call_target="tpu_custom_call" | custom-call | tf_op jit(solution)/shard_map/pallas_call | solution.py:415
  45.6 0.8 %shard_map.76 = (bf16[16,4096]{1,0:T(8,128)(2,1)}, bf16[4,4096]{1,0:T(4,128)(2,1)}, f32[8,1728]{1,0:T(8,128)}, f32[16,3456]{1,0:T(8,128)}) custom-call(bf16[16,4096]{1,0:T(8,128)(2,1)S(1)} %get-tuple-element.12.feat, bf16[4,4096]{1,0:T(4,128)(2,1)S(1)} %get-tuple-element.13.ig, f32[8,1728]{1,0:T(8,128)S(1)} %get-tuple-element.14.g1, ...), custom_call_target="tpu_custom_call" | custom-call | tf_op jit(solution)/shard_map/pallas_call | solution.py:430

commit v6 on v5

--- a/solution.py
+++ b/solution.py
@@ -245,14 +245,12 @@
             there = to * 4 + (q + 3 - 2 * side) % 4
             edge_copies.append(send(src, ghe.at[n], es.at[n], er.at[n], s, there))
     gh_copies = []
-    for half in range(2):
-        for i in (1 + 2 * half, 2 + 2 * half):
-            lanes = slice(PLANE * i, PLANE * (i + 1))
-            ghb[:, lanes] = transposed(w2s, e2, i, 128).astype(BF16)
-        lanes = slice(PLANE * (1 + 2 * half), PLANE * (3 + 2 * half))
+    for i in range(1, OWN + 1):
+        lanes = slice(PLANE * i, PLANE * (i + 1))
+        ghb[:, lanes] = transposed(w2s, e2, i, 128).astype(BF16)
         for r in (2, 1, 3):
             to = (col + r) % 4
-            n = 3 * half + r - 1
+            n = 3 * (i - 1) + r - 1
             src = ghb.at[at(to * 32, 32, 32), lanes]
             gh_copies.append(send(src, ghr.at[n], gs.at[n], gr.at[n], s, col_peer(r)))
 
@@ -278,14 +276,15 @@
         there = col * 4 + (to % 2) * 2 + core
         gp_copies.append(send(src, gpr.at[r - 1], ps.at[r - 1], pr.at[r - 1], to // 2, there))
 
-    for c in gh_copies + edge_copies:
-        c.wait_recv()
-    for p in range(OWN):
+    for p in (1, 2, 0, 3):
+        for c in gh_copies[3 * p : 3 * p + 3]:
+            c.wait_recv()
+        for c in {0: edge_copies[4:], OWN - 1: edge_copies[:4]}.get(p, []):
+            c.wait_recv()
         lanes = slice(PLANE * (p + 1), PLANE * (p + 2))
         total = ghb[rows32, lanes].astype(F32)
-        part = slice(PLANE * (p % 2), PLANE * (p % 2 + 1))
         for r in range(3):
-            total += ghr[3 * (p // 2) + r, :, part].astype(F32)
+            total += ghr[3 * p + r].astype(F32)
         for edge, side, inside in ((0, 1, q > 0), (OWN - 1, 0, q < 3)):
             if p == edge:
                 more = ghe[4 * side].astype(F32)
@@ -398,7 +397,7 @@
         V((288, 192), BF16), V((576, 384), BF16), V((64, 12 * PLANE), F32), V((192, WIDE2), BF16),
         V((288, WIDE2), F32), V((32, WIDE1), F32), V((128, WIDE1), BF16), V((384, WIDE1), BF16),
         V((576, WIDE1), F32), V((4, 16, SLAB), BF16), V((4, 16, SLAB), BF16), V((192, SLAB), BF16),
-        V((128, WIDE1), BF16), V((6, 32, 2 * PLANE), BF16), V((8, 32, PLANE), BF16),
+        V((128, WIDE1), BF16), V((12, 32, PLANE), BF16), V((8, 32, PLANE), BF16),
         V((96, SLAB), BF16), V((16, 4, WIDE1), BF16), V((16, 4, WIDE1), BF16),
         V((9, 64, 384), F32), V((2, 9, 16, 384), BF16), V((2, 9, 16, 384), BF16),
         V((2, 32, 16, 128), BF16), V((15, 4, 16, 128), BF16),
@@ -406,7 +405,7 @@
         V((8, 1728), F32), V((8, 1728), BF16), V((3, 8, 1728), BF16),
     ] + [
         dma((n,)) for n in
-        (4, 15, 15, 3, 3, 3, 3, 3, 3, 18, 18, 3, 3, 6, 6, 8, 8, 3, 3, 15, 15, 7, 7, 15, 15, 7, 7, 3, 3)
+        (4, 15, 15, 3, 3, 3, 3, 3, 3, 18, 18, 3, 3, 12, 12, 8, 8, 3, 3, 15, 15, 7, 7, 15, 15, 7, 7, 3, 3)
     ]
     hbm = pl.BlockSpec(memory_space=pltpu.HBM)
     given = (volumes.reshape(4, cells), w_first, w_second, cotangent.reshape(16, cells))

time: 46.5 us -> 46.6 us (level)
  no operation moved by 1% of the time
where the time goes in v6:
time: 46.6 us; the launch traced here: 46.5 us
  Pallas kernels  45.9 us (98%)
  between operations  0.64 us (1%)
    pallas_call x1, Pallas kernels, local_step(): pl.pallas_call(functools.partial(kernel, scale), out_shape=(jax.ShapeDtyp...  45.1 us

profile of v6, /device:TPU:1, one launch (start us, length us, event | category | flops | bytes accessed | tf_op | source)
XLA Modules:
  0.0 46.5 jit_solution(11144611097893048587)
XLA Ops:
  0.6 45.1 %shard_map.75 = (bf16[16,4096]{1,0:T(8,128)(2,1)S(1)}, bf16[4,4096]{1,0:T(4,128)(2,1)S(1)}, f32[8,1728]{1,0:T(8,128)S(1)}, bf16[32,16,128]{2,1,0:T(8,128)(2,1)S(1)}) custom-call(bf16[4,4096]{1,0:T(4,128)(2,1)} %bitcast.5, bf16[8,1728]{1,0:T(8,128)(2,1)} %w1.1, bf16[16,3456]{1,0:T(8,128)(2,1)} %w2.1, bf16[16,4096]{1,0:T(8,128)(2,1)} %bitcast.4), custom_call_target="tpu_custom_call" | custom-call | tf_op jit(solution)/shard_map/pallas_call | solution.py:414
  45.7 0.8 %shard_map.76 = (bf16[16,4096]{1,0:T(8,128)(2,1)}, bf16[4,4096]{1,0:T(4,128)(2,1)}, f32[8,1728]{1,0:T(8,128)}, f32[16,3456]{1,0:T(8,128)}) custom-call(bf16[16,4096]{1,0:T(8,128)(2,1)S(1)} %get-tuple-element.12.feat, bf16[4,4096]{1,0:T(4,128)(2,1)S(1)} %get-tuple-element.13.ig, f32[8,1728]{1,0:T(8,128)S(1)} %get-tuple-element.14.g1, ...), custom_call_target="tpu_custom_call" | custom-call | tf_op jit(solution)/shard_map/pallas_call | solution.py:429
